TPU v7x, 128 devices: a whole 4x4x4 slice. The times are simulated.
128 devices in a mesh: row: 8 (over y, core), col: 16 (over x, z).
Axes of the slice: x: 4, y: 4, z: 4, core: 2. Of those that a mesh axis runs over, the one named last changes fastest.
Arguments:
- x_slots: bfloat16 [8, 16, 128, 128, 128], P('row', 'col'), may hold values from -0.875 to 0.875
- block_pairs: int32 [8, 16], replicated, may hold values from -1 to 15, as said below
- greens: bfloat16 [2, 512, 512], replicated, may hold values from -0.25 to 0.25
- green_mask: int32 [2, 4, 4], replicated, may hold values 0 or 1
- chi_mask: int32 [8, 8], P('row'), may hold values 0 or 1
Outputs:
- chi_blocks: float32 [1024, 1024], P(('row', 'col'))
Inputs may be any that keep to these rules, and one draw needn't show every extreme that they name: `block_pairs`: in each row exactly 10 slots name basis-pair blocks, all different, and all other slots are -1; in every row, all 1 slots of some col index are named.
All inputs are finite; a program needn't handle non-finite values. No bound on the sum of `chi_mask` on one device may be relied on, other than what follows from the above.
Results may differ from a plain program's by a relative error of at most 0.0041.
Values may be sent and summed in bfloat16 or wider, within the bound.
No kernel may reach another device: no remote copies, remote signals or barrier semaphores. Data moves between devices by JAX's collectives and lax.ppermute only.
A program may use at most 64 MiB of HBM per device.

v0:
```python
import jax
import jax.numpy as jnp
from jax import lax
from jax.sharding import Mesh
from jax.sharding import PartitionSpec as P

B = 128
AB = 128
NBLK = 4
NNZ = 10
ROW = ("row_0", "row_1")
COL = ("col_0", "col_1")
ROW_COL = ("row_0", "row_1", "col_0", "col_1")


def sum_in_order(tiles, axes, order):
    inside = tiles.shape[1:]
    tiles = tiles.reshape(*(lax.axis_size(a) for a in axes), *inside)
    tiles = jnp.moveaxis(tiles, order, range(len(axes))).reshape(-1, *inside)
    for k in order:
        tiles = lax.psum_scatter(tiles, axes[k], scatter_dimension=0, tiled=True)
    return tiles[0]


def split_up(array, dim, peers):
    shape = array.shape
    tiles = array.reshape(*shape[:dim], peers, shape[dim] // peers, *shape[dim + 1 :])
    return jnp.moveaxis(tiles, dim, 0)


def scatter_axes(array, axes, order, dim):
    peers = lax.axis_size(axes)
    return sum_in_order(split_up(array, dim, peers), axes, order)


def on_device(x_slots, block_pairs, greens, green_mask, chi_mask):
    row_count = lax.axis_size(ROW)
    col_count = lax.axis_size(COL)
    dev_count = row_count * col_count
    basis_count = NBLK * B
    pair_total = NBLK * NBLK
    row_index = lax.axis_index(ROW)
    arrived = lax.all_to_all(x_slots[0], COL, split_axis=1, concat_axis=0, tiled=True)
    aux_local = arrived.shape[1]
    pair_list = lax.dynamic_index_in_dim(block_pairs, row_index, 0, keepdims=False)
    selector = (pair_list[:, None] == jnp.arange(pair_total, dtype=jnp.int32)[None, :]).astype(
        jnp.bfloat16
    )
    pair_blocks = jnp.einsum(
        "kq,kabc->qabc", selector, arrived, preferred_element_type=jnp.float32
    ).astype(jnp.bfloat16)
    dense_x = pair_blocks.reshape(NBLK, NBLK, aux_local, B, B).transpose(2, 0, 3, 1, 4)
    dense_x = dense_x.reshape(aux_local, basis_count, basis_count)
    full_mask = jnp.repeat(jnp.repeat(green_mask, B, axis=1), B, axis=2).astype(jnp.bfloat16)
    masked = greens * full_mask
    half_done = jnp.einsum(
        "ml,pmn->pln", masked[0], dense_x, preferred_element_type=jnp.float32
    ).astype(jnp.bfloat16)
    contracted = jnp.einsum(
        "pln,ns->pls", half_done, masked[1], preferred_element_type=jnp.float32
    ).astype(jnp.bfloat16)
    aux_total = dev_count * aux_local
    named_flag = (block_pairs >= 0).astype(jnp.int32)
    position = jnp.cumsum(named_flag, axis=1) - 1
    compact_hit = (position[:, None, :] == jnp.arange(NNZ, dtype=jnp.int32)[None, :, None]) & (
        named_flag[:, None, :] > 0
    )
    compact_sel = compact_hit.astype(jnp.int32)
    named_pairs = jnp.sum(compact_sel * block_pairs[:, None, :], axis=2)
    own_sel = lax.dynamic_index_in_dim(compact_sel, row_index, 0, keepdims=False).astype(
        jnp.bfloat16
    )
    block_span = B * B // dev_count
    x_compact = jnp.einsum(
        "js,sabc->ajbc", own_sel, arrived, preferred_element_type=jnp.float32
    ).astype(jnp.bfloat16)
    image_blocks = contracted.reshape(aux_local, NBLK, B, NBLK, B).transpose(0, 1, 3, 2, 4)
    image_blocks = image_blocks.reshape(aux_local, pair_total, dev_count, block_span)
    image_rows, compact_rows = (
        lax.all_to_all(image_blocks, ROW_COL, split_axis=2, concat_axis=0, tiled=True),
        lax.all_to_all(x_compact, ROW_COL, split_axis=2, concat_axis=0, tiled=True),
    )
    expand = (
        named_pairs[:, :, None] == jnp.arange(pair_total, dtype=jnp.int32)[None, None, :]
    ).astype(jnp.bfloat16)
    compact_rows = compact_rows.reshape(row_count, aux_total // row_count, NNZ, block_span)
    dense_rows = jnp.einsum(
        "rjk,rqjz->rqkz", expand, compact_rows, preferred_element_type=jnp.float32
    ).astype(jnp.bfloat16)
    image_rows = image_rows.reshape(aux_total, pair_total * block_span)
    dense_rows = dense_rows.reshape(aux_total, pair_total * block_span)
    chi_rows = scatter_axes(
        lax.dot_general(
            image_rows, dense_rows, (((1,), (1,)), ((), ())), preferred_element_type=jnp.float32
        ),
        ROW_COL,
        (1, 0, 2, 3),
        0,
    )
    column_mask = jnp.repeat(chi_mask[0], AB).astype(jnp.float32)
    return chi_rows * column_mask[None, :]


def solution(mesh):
    split = Mesh(mesh.devices.reshape(4, 2, 4, 4), ("row_0", "row_1", "col_0", "col_1"))
    placed = (P(ROW, COL, None, None, None), P(), P(), P(), P(ROW, None))
    return jax.shard_map(
        on_device, mesh=split, in_specs=placed, out_specs=P(ROW_COL, None), check_vma=False
    )
```

profile of v0, /device:TPU:0, one launch (start us, length us, event | category | flops | bytes accessed | tf_op | source)
XLA Modules:
  0.0 326.9 jit_solution(11970308047859366336)
XLA Ops:
  6.5 0.0 copy-start
  6.5 8.2 %all-to-all-start = ((bf16[1,128,128,128]{3,2,0,1:T(8,128)(2,1)}), bf16[1,128,128,128]{3,2,0,1:T(8,128)(2,1)}, u32[]{:S(2)}, u32[]{:S(2)}) async-start(bf16[1,128,128,128]{3,2,0,1:T(8,128)(2,1)} %bitcast.82), calls=%async_computation | async-start | bytes 8388608 | tf_op jit(solution)/shard_map/all_to_all | solution.py:43
  14.7 0.0 copy-done
  14.7 0.2 reduce_window_sum.11
  14.9 61.6 %all-to-all-done = bf16[1,128,128,128]{3,2,0,1:T(8,128)(2,1)} async-done(((bf16[1,128,128,128]{3,2,0,1:T(8,128)(2,1)}), bf16[1,128,128,128]{3,2,0,1:T(8,128)(2,1)}, u32[]{:S(2)}, u32[]{:S(2)}) %all-to-all-start) | async-done | bytes 4194336 | tf_op jit(solution)/shard_map/all_to_all | solution.py:43
  76.6 5.0 %convert_bitcast_fusion.1 = bf16[8,10,128,128]{3,1,2,0:T(8,128)(2,1)S(1)} fusion(bf16[16,8,128,128]{3,2,1,0:T(8,128)(2,1)} %bitcast.4, pred[8,10,16]{2,1,0:T(8,128)(4,1)S(1)} %fusion.26, s32[]{:T(128)S(6)} %select_n.6), kind=kOutput, calls=%fused_computation.8 | convolution fusion | flops 43254080 | bytes 6817796 | tf_op jit(solution)/shard_map/js,sabc->ajbc/dot_general | solution.py:74
  81.5 4.6 %copy.21 = bf16[8,10,128,128]{3,0,1,2:T(8,128)(2,1)} copy(bf16[8,10,128,128]{3,1,2,0:T(8,128)(2,1)S(1)} %convert_bitcast_fusion.1) | data formatting | bytes 5242880 | tf_op jit(solution)/shard_map/convert_element_type | solution.py:76
  86.1 0.0 copy-start.1
  86.1 14.6 %all-to-all-start.2 = ((bf16[8,10,128,128]{3,0,1,2:T(8,128)(2,1)}), bf16[8,10,128,128]{3,0,1,2:T(8,128)(2,1)S(1)}, u32[]{:S(2)}, u32[]{:S(2)}) async-start(bf16[8,10,128,128]{3,0,1,2:T(8,128)(2,1)} %copy.21), calls=%async_computation.2 | async-start | bytes 5242880 | tf_op jit(solution)/shard_map/all_to_all | solution.py:81
  100.7 0.0 copy-done.1
  100.8 2.1 broadcast_in_dim.7
  102.9 2.2 convert_element_type.66
  105.1 2.8 mul.23
  107.9 5.0 %fusion.11 = bf16[16,8,128,128]{3,0,2,1:T(8,128)(2,1)S(1)} fusion(bf16[16,8,128,128]{3,2,1,0:T(8,128)(2,1)} %bitcast.4, s32[16]{0:T(128)S(1)} %dynamic-slice_bitcast_fusion), kind=kOutput, calls=%fused_computation.14 | convolution fusion | flops 69206272 | bytes 8388672 | tf_op jit(solution)/shard_map/kq,kabc->qabc/dot_general | solution.py:49
  112.9 4.3 %copy.44 = bf16[4,4,8,128,128]{4,1,3,0,2:T(4,128)(2,1)} copy(bf16[4,4,8,128,128]{4,1,0,3,2:T(4,128)(2,1)S(1)} %bitcast.79) | data formatting | bytes 8388608 | tf_op jit(solution)/shard_map/reshape | solution.py:52
  117.1 7.2 %reshape.56 = bf16[8,512,512]{2,1,0:T(8,128)(2,1)} reshape(bf16[8,4,128,4,128]{4,3,2,1,0:T(4,128)(2,1)} %bitcast.80) | data formatting | bytes 8388608 | tf_op jit(solution)/shard_map/reshape | solution.py:53
  124.3 9.0 %fusion.18 = bf16[8,512,512]{2,1,0:T(8,128)(2,1)} fusion(bf16[8,512,512]{2,1,0:T(8,128)(2,1)} %reshape.56, bf16[2,512,512]{2,1,0:T(8,128)(2,1)} %mul.23), kind=kOutput, calls=%fused_computation.15 | convolution fusion | flops 4299161600 | bytes 9437184 | tf_op jit(solution)/shard_map/pln,ns->pls/dot_general | solution.py:59
  133.3 6.9 %reshape.57 = bf16[8,4,128,4,128]{4,3,2,1,0:T(4,128)(2,1)} reshape(bf16[8,512,512]{2,1,0:T(8,128)(2,1)} %fusion.18) | data formatting | bytes 8388608 | tf_op jit(solution)/shard_map/reshape | solution.py:77
  140.2 3.3 %copy.18 = bf16[8,4,128,4,128]{4,2,3,1,0:T(8,128)(2,1)S(1)} copy(bf16[8,4,128,4,128]{4,3,2,1,0:T(4,128)(2,1)} %reshape.57) | data formatting | bytes 8388608 | tf_op jit(solution)/shard_map/reshape | solution.py:77
  143.6 4.7 %copy.19 = bf16[8,16,128,128]{3,1,0,2:T(8,128)(2,1)} copy(bf16[8,16,128,128]{3,2,1,0:T(8,128)(2,1)S(1)} %bitcast.81) | data formatting | bytes 8388608 | tf_op jit(solution)/shard_map/reshape | solution.py:78
  148.2 0.0 all-to-all-done.2
  148.2 10.1 %all-to-all-start.1 = ((bf16[8,16,128,128]{3,1,0,2:T(8,128)(2,1)}), bf16[8,16,128,128]{3,1,0,2:T(8,128)(2,1)}, u32[]{:S(2)}, u32[]{:S(2)}) async-start(bf16[8,16,128,128]{3,1,0,2:T(8,128)(2,1)} %copy.19), calls=%async_computation.1 | async-start | bytes 8388608 | tf_op jit(solution)/shard_map/all_to_all | solution.py:80
  158.4 0.0 reduce-scatter.5.cloned.1.call-start
  158.4 0.2 select_reduce_fusion
  158.6 0.6 copy.22
  159.2 3.9 %convert_bitcast_fusion = bf16[8,128,16,128]{3,2,1,0:T(8,128)(2,1)} fusion(bf16[8,128,10,128]{3,1,0,2:T(8,128)(2,1)S(1)} %bitcast.77, s32[8,10]{1,0:T(8,128)S(1)} %select_reduce_fusion), kind=kOutput, calls=%fused_computation.7 | convolution fusion | flops 44041472 | bytes 6816064 | tf_op jit(solution)/shard_map/rjk,rqjz->rqkz/dot_general | solution.py:87
  163.1 7.3 %reshape.67 = bf16[1024,2048,1,1,1,1]{1,0,2,3,4,5:T(8,128)(2,1)} reshape(bf16[8,128,16,128]{3,2,1,0:T(8,128)(2,1)} %convert_bitcast_fusion) | data formatting | bytes 8388608 | tf_op jit(solution)/shard_map/reshape | solution.py:91
  170.4 39.4 %all-to-all-done.1 = bf16[8,16,128,128]{3,1,0,2:T(8,128)(2,1)} async-done(((bf16[8,16,128,128]{3,1,0,2:T(8,128)(2,1)}), bf16[8,16,128,128]{3,1,0,2:T(8,128)(2,1)}, u32[]{:S(2)}, u32[]{:S(2)}) %all-to-all-start.1) | async-done | bytes 4194336 | tf_op jit(solution)/shard_map/all_to_all | solution.py:80
  209.8 7.3 %dot_general.23 = bf16[4,2,4,4,8,2048]{5,4,3,2,1,0:T(8,128)(2,1)} reshape(bf16[128,8,16,1,128]{4,2,1,0,3:T(8,128)(2,1)} %bitcast.16) | data formatting | bytes 8388608 | tf_op jit(solution)/shard_map/dot_general | solution.py:93
  217.2 7.6 %fusion.21 = f32[2,4,4,4,8,1024]{5,4,3,2,0,1:T(8,128)S(1)} fusion(bf16[4,2,4,4,8,2048]{5,4,3,2,1,0:T(8,128)(2,1)} %dot_general.23, bf16[1024,2048,1,1,1,1]{1,0,2,3,4,5:T(8,128)(2,1)} %reshape.67), kind=kOutput, calls=%fused_computation.16 | convolution fusion | flops 4294967296 | bytes 12582912 | tf_op jit(solution)/shard_map/dot_general | solution.py:93
  224.8 2.5 copy.24
  227.3 0.0 copy-start.2
  227.3 0.0 reduce-scatter.5.cloned.1.call-update
  227.3 0.0 reduce-scatter.7.cloned.1.call-start
  227.4 11.3 %reduce-scatter.5.cloned.1.call-done = f32[64,8,1024]{2,1,0:T(8,128)} async-done(((f32[128,8,1024]{2,1,0:T(8,128)}), f32[64,8,1024]{2,1,0:T(8,128)}) %reduce-scatter.5.cloned.1.call-update) | async-done | bytes 2097168 | tf_op jit(solution)/shard_map/reduce_scatter | solution.py:21
  238.7 0.0 reduce-scatter.7.cloned.1.call-update
  238.7 0.0 reduce-scatter.9.cloned.1.call-start
  238.8 33.5 %reduce-scatter.7.cloned.1.call-done = f32[16,8,1024]{2,1,0:T(8,128)} async-done(((f32[64,8,1024]{2,1,0:T(8,128)}), f32[16,8,1024]{2,1,0:T(8,128)}) %reduce-scatter.7.cloned.1.call-update) | async-done | bytes 524304 | tf_op jit(solution)/shard_map/reduce_scatter | solution.py:21
  272.2 0.0 reduce-scatter.9.cloned.1.call-update
  272.2 0.0 reduce-scatter.11.cloned.1.call-start
  272.3 23.7 %reduce-scatter.9.cloned.1.call-done = f32[4,8,1024]{2,1,0:T(8,128)} async-done(((f32[16,8,1024]{2,1,0:T(8,128)}), f32[4,8,1024]{2,1,0:T(8,128)}) %reduce-scatter.9.cloned.1.call-update) | async-done | bytes 131088 | tf_op jit(solution)/shard_map/reduce_scatter | solution.py:21
  296.0 0.0 reduce-scatter.11.cloned.1.call-update
  296.0 0.0 copy-done.2
  296.0 0.1 broadcast_bitcast_fusion
  296.1 22.9 %reduce-scatter.11.cloned.1.call-done = f32[1,8,1024]{2,1,0:T(8,128)} async-done(((f32[4,8,1024]{2,1,0:T(8,128)}), f32[1,8,1024]{2,1,0:T(8,128)}) %reduce-scatter.11.cloned.1.call-update) | async-done | bytes 32784 | tf_op jit(solution)/shard_map/reduce_scatter | solution.py:21
  319.0 1.4 bitcast_multiply_fusion
  (7 shorter events, 0.1 us)
Async XLA Ops:
  6.5 8.2 %copy-start = (s32[8,16]{1,0:T(8,128)S(1)}, s32[8,16]{1,0:T(8,128)}, u32[]{:S(2)}) copy-start(s32[8,16]{1,0:T(8,128)} %param.6) | copy-start | bytes 1540
  6.5 70.0 %all-to-all-start = ((bf16[1,128,128,128]{3,2,0,1:T(8,128)(2,1)}), bf16[1,128,128,128]{3,2,0,1:T(8,128)(2,1)}, u32[]{:S(2)}, u32[]{:S(2)}) async-start(bf16[1,128,128,128]{3,2,0,1:T(8,128)(2,1)} %bitcast.82), calls=%async_computation | async-start | bytes 8388608 | tf_op jit(solution)/shard_map/all_to_all | solution.py:43
  86.1 14.6 %copy-start.1 = (s32[2,4,4]{2,1,0:T(4,128)S(1)}, s32[2,4,4]{2,1,0:T(4,128)}, u32[]{:S(2)}) copy-start(s32[2,4,4]{2,1,0:T(4,128)} %param.8) | copy-start | bytes 388
  86.1 62.1 %all-to-all-start.2 = ((bf16[8,10,128,128]{3,0,1,2:T(8,128)(2,1)}), bf16[8,10,128,128]{3,0,1,2:T(8,128)(2,1)S(1)}, u32[]{:S(2)}, u32[]{:S(2)}) async-start(bf16[8,10,128,128]{3,0,1,2:T(8,128)(2,1)} %copy.21), calls=%async_computation.2 | async-start | bytes 5242880 | tf_op jit(solution)/shard_map/all_to_all | solution.py:81
  148.2 61.6 %all-to-all-start.1 = ((bf16[8,16,128,128]{3,1,0,2:T(8,128)(2,1)}), bf16[8,16,128,128]{3,1,0,2:T(8,128)(2,1)}, u32[]{:S(2)}, u32[]{:S(2)}) async-start(bf16[8,16,128,128]{3,1,0,2:T(8,128)(2,1)} %copy.19), calls=%async_computation.1 | async-start | bytes 8388608 | tf_op jit(solution)/shard_map/all_to_all | solution.py:80
  158.4 80.3 %reduce-scatter.5.cloned.1.call-start = ((), (), s32[]{:S(2)}) async-start(), calls=%async_computation.7 | async-start | bytes 6291456 | tf_op jit(solution)/shard_map/reduce_scatter | solution.py:21
  227.3 68.7 %copy-start.2 = (s32[1,8]{1,0:T(1,128)S(1)}, s32[1,8]{1,0:T(1,128)}, u32[]{:S(2)}) copy-start(s32[1,8]{1,0:T(1,128)} %param.9) | copy-start | bytes 100
  227.3 44.9 %reduce-scatter.7.cloned.1.call-start = ((), (), s32[]{:S(2)}) async-start(), calls=%async_computation.8 | async-start | bytes 2621440 | tf_op jit(solution)/shard_map/reduce_scatter | solution.py:21
  238.7 57.3 %reduce-scatter.9.cloned.1.call-start = ((), (), s32[]{:S(2)}) async-start(), calls=%async_computation.9 | async-start | bytes 655360 | tf_op jit(solution)/shard_map/reduce_scatter | solution.py:21
  272.2 46.7 %reduce-scatter.11.cloned.1.call-start = ((), (), s32[]{:S(2)}) async-start(), calls=%async_computation.10 | async-start | bytes 163840 | tf_op jit(solution)/shard_map/reduce_scatter | solution.py:21
Sparse Core Ops, SparseCore 0:
  227.4 11.2 reduce-scatter.4
  241.1 31.0 reduce-scatter.6
  274.6 21.3 reduce-scatter.8
  298.2 20.7 reduce-scatter.10
where the time goes:
time: 328 us; the launch traced here: 327 us
  waiting for transfers between devices  192 us (59%)
  local copies, waits for them, and re-layouts  53.1 us (16%)
  starting transfers between devices  33.1 us (10%)
  matrix products  30.4 us (9%)
  between operations  13.3 us (4%)
  other arithmetic  4.61 us (1%)
    reduce_scatter x4, waiting for transfers between devices, sum_in_order(): tiles = lax.psum_scatter(tiles, axes[k], scatter_dimension=0, tiled=True)  91.3 us
    all_to_all x1, waiting for transfers between devices, on_device(): lax.all_to_all(x_slots[0], COL, split_axis=1, concat_axis=0, tiled=True)  61.6 us
    all_to_all x1, waiting for transfers between devices, on_device(): lax.all_to_all(image_blocks, ROW_COL, split_axis=2, concat_axis=0, tiled=...  39.4 us
    all_to_all x1, starting transfers between devices, on_device(): lax.all_to_all(x_compact, ROW_COL, split_axis=2, concat_axis=0, tiled=True)  14.6 us
    reshape x2, local copies, waits for them, and re-layouts, on_device(): contracted.reshape(aux_local, NBLK, B, NBLK, B).transpose(0, 1, 3, 2, 4)  10.2 us
    all_to_all x1, starting transfers between devices, on_device(): lax.all_to_all(image_blocks, ROW_COL, split_axis=2, concat_axis=0, tiled=...  10.1 us
    dot_general x1, matrix products, on_device(): jnp.einsum('pln,ns->pls', half_done, masked[1], preferred_element_type=jn...  8.99 us
    all_to_all x1, starting transfers between devices, on_device(): lax.all_to_all(x_slots[0], COL, split_axis=1, concat_axis=0, tiled=True)  8.17 us
  transfers between devices with their start and end apart: 7, of which 6 were waited for; matrix products, arithmetic and copies ran while one was open for 18% of the time, Pallas kernels for 0%

commit v1 on v0

v1 whole, which is shorter than its diff:
```python
import jax
import jax.numpy as jnp
from jax import lax
from jax.experimental import pallas as pl
from jax.experimental.pallas import tpu as pltpu
from jax.sharding import Mesh
from jax.sharding import PartitionSpec as P

B = 128
AB = 128
NBLK = 4
NPAIR = NBLK * NBLK
NBAS = NBLK * B
NNZ = 10
N_ROW = 8
N_COL = 16
AUX = AB // N_COL
NCHIP = 64
SUB = B // NCHIP
SPAN = SUB * B
ROWS = NCHIP * AUX
VMEM_LIMIT = 60 * 1024 * 1024


def named_kernel(slot_of_ref, arrived_ref, out_ref, scratch):
    for aux in range(AUX):
        for j in range(NNZ):
            block = arrived_ref[slot_of_ref[j], aux].astype(jnp.float32)
            for sub in range(SUB):
                scratch[j * SUB + sub, pl.ds(aux, NCHIP, stride=AUX), :] = block[
                    sub * NCHIP : (sub + 1) * NCHIP
                ]
    for k in range(NNZ * SUB):
        out_ref[:, k * B : (k + 1) * B] = scratch[k].astype(jnp.bfloat16)


def named_slices(slot_of, arrived):
    return pl.pallas_call(
        named_kernel,
        out_shape=jax.ShapeDtypeStruct((ROWS, NNZ * SPAN), jnp.bfloat16),
        grid_spec=pltpu.PrefetchScalarGridSpec(
            num_scalar_prefetch=1,
            grid=(),
            in_specs=[pl.BlockSpec(memory_space=pltpu.VMEM)],
            out_specs=pl.BlockSpec(memory_space=pltpu.VMEM),
            scratch_shapes=[pltpu.VMEM((NNZ * SUB, ROWS, B), jnp.float32)],
        ),
        compiler_params=pltpu.CompilerParams(vmem_limit_bytes=VMEM_LIMIT),
        name="named_slices",
    )(slot_of, arrived)


def contract_kernel(block_slot_ref, arrived_ref, occ_t_ref, virt_ref, out_ref, scratch, dense):
    def one(aux, carry):
        for m in range(NBLK):
            for n in range(NBLK):
                slot = block_slot_ref[m * NBLK + n]
                block = arrived_ref[jnp.maximum(slot, 0), aux]
                keep = jnp.where(slot >= 0, 1.0, 0.0)
                block = jnp.where(keep > 0.5, block.astype(jnp.float32), 0.0).astype(jnp.bfloat16)
                dense[m * B : (m + 1) * B, n * B : (n + 1) * B] = block
        half = jnp.dot(
            occ_t_ref[...], dense[...], preferred_element_type=jnp.float32
        ).astype(jnp.bfloat16)
        full = jnp.dot(half, virt_ref[...], preferred_element_type=jnp.float32)
        for m in range(NBLK):
            for sub in range(SUB):
                row = m * B + sub * NCHIP
                for n in range(NBLK):
                    scratch[(m * NBLK + n) * SUB + sub, pl.ds(aux, NCHIP, stride=AUX), :] = full[
                        row : row + NCHIP, n * B : (n + 1) * B
                    ]
        return carry

    lax.fori_loop(0, AUX, one, 0)
    for k in range(NPAIR * SUB):
        out_ref[:, k * B : (k + 1) * B] = scratch[k].astype(jnp.bfloat16)


def contracted_slices(block_slot, arrived, occ_t, virt):
    return pl.pallas_call(
        contract_kernel,
        out_shape=jax.ShapeDtypeStruct((ROWS, NPAIR * SPAN), jnp.bfloat16),
        grid_spec=pltpu.PrefetchScalarGridSpec(
            num_scalar_prefetch=1,
            grid=(),
            in_specs=[pl.BlockSpec(memory_space=pltpu.VMEM)] * 3,
            out_specs=pl.BlockSpec(memory_space=pltpu.VMEM),
            scratch_shapes=[
                pltpu.VMEM((NPAIR * SUB, ROWS, B), jnp.float32),
                pltpu.VMEM((NBAS, NBAS), jnp.bfloat16),
            ],
        ),
        compiler_params=pltpu.CompilerParams(vmem_limit_bytes=VMEM_LIMIT),
        name="contracted_slices",
    )(block_slot, arrived, occ_t, virt)


def chi_kernel(pairs_ref, core_ref, image_ref, own_ref, other_ref, out_ref):
    core = core_ref[0]
    for y in range(N_ROW // 2):
        for ref, side in ((own_ref, core), (other_ref, 1 - core)):
            row = 2 * y + side
            total = jnp.zeros((ROWS, AB), jnp.float32)
            for j in range(NNZ):
                start = pl.multiple_of(pairs_ref[row, j] * SPAN, SPAN)
                total += lax.dot_general(
                    image_ref[:, pl.ds(start, SPAN)],
                    ref[y * AB : (y + 1) * AB, j * SPAN : (j + 1) * SPAN],
                    (((1,), (1,)), ((), ())),
                    preferred_element_type=jnp.float32,
                )
            out_ref[:, pl.ds(pl.multiple_of(row * AB, AB), AB)] = total.astype(jnp.bfloat16)


def chi_partials(pairs, core, image, own, other):
    return pl.pallas_call(
        chi_kernel,
        out_shape=jax.ShapeDtypeStruct((ROWS, N_ROW * AB), jnp.bfloat16),
        grid_spec=pltpu.PrefetchScalarGridSpec(
            num_scalar_prefetch=2,
            grid=(),
            in_specs=[pl.BlockSpec(memory_space=pltpu.VMEM)] * 3,
            out_specs=pl.BlockSpec(memory_space=pltpu.VMEM),
        ),
        compiler_params=pltpu.CompilerParams(vmem_limit_bytes=VMEM_LIMIT),
        name="chi_partials",
    )(pairs, core, image, own, other)


def on_device(x_slots, block_pairs, greens, green_mask, chi_mask):
    core = lax.axis_index("c").astype(jnp.int32)
    row = lax.axis_index(("y", "c"))
    chips = ("y", "x", "z")
    named = (block_pairs >= 0).astype(jnp.int32)
    place = jnp.cumsum(named, axis=1) - 1
    hit = (place[:, None, :] == jnp.arange(NNZ)[None, :, None]) & (named[:, None, :] > 0)
    pairs = jnp.sum(jnp.where(hit, block_pairs[:, None, :], 0), axis=2)
    own_hit = lax.dynamic_index_in_dim(hit, row, 0, keepdims=False)
    slot_ids = jnp.arange(N_COL, dtype=jnp.int32)
    slot_of = jnp.sum(jnp.where(own_hit, slot_ids[None, :], 0), axis=1)
    own_pairs = lax.dynamic_index_in_dim(block_pairs, row, 0, keepdims=False)
    at_block = own_pairs[None, :] == jnp.arange(NPAIR, dtype=jnp.int32)[:, None]
    block_slot = jnp.sum(jnp.where(at_block, slot_ids[None, :] + 1, 0), axis=1) - 1

    masked = greens.reshape(2, NBLK, B, NBLK, B) * green_mask.astype(jnp.bfloat16)[
        :, :, None, :, None
    ]
    masked = masked.reshape(2, NBAS, NBAS)
    occ_t = masked[0].T
    virt = masked[1]

    arrived = lax.all_to_all(
        x_slots[0, 0].reshape(N_COL, AUX, B, B), ("x", "z"), 0, 0, tiled=True
    )
    own = named_slices(slot_of, arrived)
    own = lax.all_to_all(
        own.reshape(NCHIP, AUX, NNZ * SPAN), chips, 0, 0, tiled=True
    ).reshape(ROWS, NNZ * SPAN)
    other = lax.ppermute(own, "c", [(0, 1), (1, 0)])
    image = contracted_slices(block_slot, arrived, occ_t, virt)
    image = lax.all_to_all(
        image.reshape(NCHIP, AUX, NPAIR * SPAN), chips, 0, 0, tiled=True
    ).reshape(ROWS, NPAIR * SPAN)
    part = chi_partials(pairs, core[None], image, own, other)
    part = lax.all_to_all(part.reshape(NCHIP, AUX, N_ROW * AB), chips, 0, 0, tiled=True)
    chi = jnp.sum(part.astype(jnp.float32), axis=0)
    return chi * jnp.repeat(chi_mask[0], AB).astype(jnp.float32)[None, :]


def solution(mesh):
    split = Mesh(mesh.devices.reshape(4, 2, 4, 4), ("y", "c", "x", "z"))
    row, col = ("y", "c"), ("x", "z")
    placed = (P(row, col, None, None, None), P(), P(), P(), P(row, None))
    return jax.shard_map(
        on_device,
        mesh=split,
        in_specs=placed,
        out_specs=P(row + col, None),
        check_vma=False,
    )
```

time: 328 us -> 221 us (0.67)
  waiting for transfers between devices: 192 us -> 140 us
  local copies, waits for them, and re-layouts: 53.1 us -> 4.57 us
  Pallas kernels: 0 us -> 31.3 us
  matrix products: 30.4 us -> 0 us
  between operations: 13.3 us -> 0.13 us
  starting transfers between devices: 33.1 us -> 40 us
    reduce_scatter x4 -> x0, waiting for transfers between devices: 91.3 us -> none  [sum_in_order(): tiles = lax.psum_scatter(tiles, axes[k], scatter_dimension=0, tiled=True)]
    all_to_all x3 -> x4, waiting for transfers between devices: 101 us -> 140 us  [the longest x1 61 us: on_device(): lax.all_to_all(x_slots[0, 0].reshape(N_COL, AUX, B, B), ('x', 'z'), 0, 0,...]
    reshape x6 -> x1, local copies, waits for them, and re-layouts: 33.7 us -> 2.15 us  [on_device(): greens.reshape(2, NBLK, B, NBLK, B)]
    pallas_call x0 -> x3, Pallas kernels: none -> 31.3 us  [the longest x1 13.7 us: contracted_slices(): pl.pallas_call(contract_kernel, out_shape=jax.ShapeDtypeStruct((ROWS, NPA...]
    dot_general x5 -> x0, matrix products: 30.4 us -> none  [the longest x1 8.99 us: on_device(): jnp.einsum('pln,ns->pls', half_done, masked[1], preferred_element_type=jn...]
    dot_general x1 -> x0, local copies, waits for them, and re-layouts: 7.33 us -> none  [on_device(): lax.dot_general(image_rows, dense_rows, (((1,), (1,)), ((), ())), preferr...]
    all_to_all x3 -> x4, starting transfers between devices: 32.9 us -> 39.9 us  [the longest x1 14.9 us: on_device(): lax.all_to_all(own.reshape(NCHIP, AUX, NNZ * SPAN), chips, 0, 0, tiled=True)]
    convert_element_type x3 -> x1, local copies, waits for them, and re-layouts: 6.91 us -> 0.07 us  [on_device(): return chi * jnp.repeat(chi_mask[0], AB).astype(jnp.float32)[None, :]]
  transfers between devices with their start and end apart: 7 -> 5, of which waited for: 6 -> 4; matrix products, arithmetic and copies ran while one was open for 18% -> 4% of each run, Pallas kernels for 0% -> 6%
where the time goes in v1:
time: 221 us; the launch traced here: 220 us
  waiting for transfers between devices  140 us (63%)
  starting transfers between devices  40 us (18%)
  Pallas kernels  31.3 us (14%)
  other arithmetic  4.83 us (2%)
  local copies, waits for them, and re-layouts  4.57 us (2%)
    all_to_all x1, waiting for transfers between devices, on_device(): lax.all_to_all(x_slots[0, 0].reshape(N_COL, AUX, B, B), ('x', 'z'), 0, 0,...  61 us
    all_to_all x1, waiting for transfers between devices, on_device(): lax.all_to_all(image.reshape(NCHIP, AUX, NPAIR * SPAN), chips, 0, 0, tile...  50.1 us
    all_to_all x1, waiting for transfers between devices, on_device(): lax.all_to_all(part.reshape(NCHIP, AUX, N_ROW * AB), chips, 0, 0, tiled=T...  15.5 us
    all_to_all x1, starting transfers between devices, on_device(): lax.all_to_all(own.reshape(NCHIP, AUX, NNZ * SPAN), chips, 0, 0, tiled=True)  14.9 us
    pallas_call x1, Pallas kernels, contracted_slices(): pl.pallas_call(contract_kernel, out_shape=jax.ShapeDtypeStruct((ROWS, NPA...  13.7 us
    all_to_all x1, waiting for transfers between devices, on_device(): lax.all_to_all(own.reshape(NCHIP, AUX, NNZ * SPAN), chips, 0, 0, tiled=True)  13.1 us
    pallas_call x1, Pallas kernels, chi_partials(): pl.pallas_call(chi_kernel, out_shape=jax.ShapeDtypeStruct((ROWS, N_ROW *...  11.3 us
    all_to_all x1, starting transfers between devices, on_device(): lax.all_to_all(part.reshape(NCHIP, AUX, N_ROW * AB), chips, 0, 0, tiled=T...  11.2 us
  transfers between devices with their start and end apart: 5, of which 4 were waited for; matrix products, arithmetic and copies ran while one was open for 4% of the time, Pallas kernels for 6%

profile of v1, /device:TPU:0, one launch (start us, length us, event | category | flops | bytes accessed | tf_op | source)
XLA Modules:
  0.0 220.5 jit_solution(10918672385285933220)
XLA Ops:
  0.0 0.0 copy-start.1
  0.0 8.2 %all-to-all-start = ((bf16[16,8,128,128]{3,2,1,0:T(8,128)(2,1)}), bf16[16,8,128,128]{3,2,1,0:T(8,128)(2,1)}, u32[]{:S(2)}, u32[]{:S(2)}) async-start(bf16[16,8,128,128]{3,2,1,0:T(8,128)(2,1)} %bitcast.31), calls=%async_computation | async-start | bytes 8388608 | tf_op jit(solution)/shard_map/all_to_all | solution.py:153
  8.2 0.0 copy-done.1
  8.2 0.2 reduce_window_sum.11
  8.4 0.6 select_reduce_fusion.1.slot_of_ref
  9.0 61.0 %all-to-all-done.arrived_ref = bf16[16,8,128,128]{3,2,1,0:T(8,128)(2,1)} async-done(((bf16[16,8,128,128]{3,2,1,0:T(8,128)(2,1)}), bf16[16,8,128,128]{3,2,1,0:T(8,128)(2,1)}, u32[]{:S(2)}, u32[]{:S(2)}) %all-to-all-start) | async-done | bytes 4194336 | tf_op jit(solution)/shard_map/all_to_all | solution.py:153
  70.0 6.3 %named_slices.1 = bf16[512,2560]{1,0:T(8,128)(2,1)} custom-call(s32[10]{0:T(128)} %select_reduce_fusion.1.slot_of_ref, bf16[16,8,128,128]{3,2,1,0:T(8,128)(2,1)} %all-to-all-done.arrived_ref), custom_call_target="tpu_custom_call" | custom-call | tf_op jit(solution)/shard_map/named_slices/pallas_call | solution.py:38
  76.3 0.0 copy-start.2
  76.3 14.9 %all-to-all-start.2 = ((bf16[64,8,2560]{2,1,0:T(8,128)(2,1)}), bf16[64,8,2560]{2,1,0:T(8,128)(2,1)S(1)}, u32[]{:S(2)}, u32[]{:S(2)}) async-start(bf16[64,8,2560]{2,1,0:T(8,128)(2,1)} %bitcast.27), calls=%async_computation.2 | async-start | bytes 5242880 | tf_op jit(solution)/shard_map/all_to_all | solution.py:157
  91.2 0.0 copy-done.2
  91.2 2.1 reshape.47
  93.4 1.7 broadcast_multiply_fusion
  95.1 0.4 fusion.1
  95.5 0.9 copy.18
  96.4 0.1 copy.19
  96.5 1.0 copy.12
  97.5 0.1 select_reduce_fusion.2
  97.6 0.5 broadcast_add_fusion.1.block_slot_ref
  98.1 13.7 %contracted_slices.1 = bf16[512,4096]{1,0:T(8,128)(2,1)} custom-call(s32[16]{0:T(128)} %broadcast_add_fusion.1.block_slot_ref, bf16[16,8,128,128]{3,2,1,0:T(8,128)(2,1)} %all-to-all-done.arrived_ref, bf16[512,512]{1,0:T(8,128)(2,1)} %bitcast.33, bf16[512,512]{1,0:T(8,128)(2,1)} %bitcast.32), custom_call_target="tpu_custom_call" | custom-call | tf_op jit(solution)/shard_map/contracted_slices/pallas_call | solution.py:81
  111.9 13.1 %all-to-all-done.2 = bf16[64,8,2560]{2,1,0:T(8,128)(2,1)S(1)} async-done(((bf16[64,8,2560]{2,1,0:T(8,128)(2,1)}), bf16[64,8,2560]{2,1,0:T(8,128)(2,1)S(1)}, u32[]{:S(2)}, u32[]{:S(2)}) %all-to-all-start.2) | async-done | bytes 2621472 | tf_op jit(solution)/shard_map/all_to_all | solution.py:157
  124.9 0.0 copy-start
  124.9 5.7 %all-to-all-start.1 = ((bf16[64,8,4096]{2,1,0:T(8,128)(2,1)}), bf16[64,8,4096]{2,1,0:T(8,128)(2,1)}, u32[]{:S(2)}, u32[]{:S(2)}) async-start(bf16[64,8,4096]{2,1,0:T(8,128)(2,1)} %bitcast.26), calls=%async_computation.1 | async-start | bytes 8388608 | tf_op jit(solution)/shard_map/all_to_all | solution.py:162
  130.6 0.0 copy-done
  130.6 0.1 collective-permute-start
  130.7 0.8 select_reduce_fusion.pairs_ref
  131.5 50.1 %all-to-all-done.1 = bf16[64,8,4096]{2,1,0:T(8,128)(2,1)} async-done(((bf16[64,8,4096]{2,1,0:T(8,128)(2,1)}), bf16[64,8,4096]{2,1,0:T(8,128)(2,1)}, u32[]{:S(2)}, u32[]{:S(2)}) %all-to-all-start.1) | async-done | bytes 4194336 | tf_op jit(solution)/shard_map/all_to_all | solution.py:162
  181.6 0.0 collective-permute-done.other_ref
  181.6 0.0 copy-start.3
  181.6 11.3 %chi_partials.1 = bf16[512,1024]{1,0:T(8,128)(2,1)} custom-call(s32[8,10]{1,0:T(8,128)} %select_reduce_fusion.pairs_ref, s32[1]{0:T(128)} %bitcast.core_ref, bf16[512,4096]{1,0:T(8,128)(2,1)} %bitcast.5.image_ref, bf16[512,2560]{1,0:T(8,128)(2,1)} %bitcast.29, bf16[512,2560]{1,0:T(8,128)(2,1)} %collective-permute-done.other_ref), custom_call_target="tpu_custom_call" | custom-call | tf_op jit(solution)/shard_map/chi_partials/pallas_call | solution.py:117
  192.9 11.2 %all-to-all-start.3 = ((bf16[64,8,1024]{2,1,0:T(8,128)(2,1)}), bf16[64,8,1024]{2,1,0:T(8,128)(2,1)S(1)}, u32[]{:S(2)}, u32[]{:S(2)}) async-start(bf16[64,8,1024]{2,1,0:T(8,128)(2,1)} %bitcast.30), calls=%async_computation.3 | async-start | bytes 2097152 | tf_op jit(solution)/shard_map/all_to_all | solution.py:166
  204.1 0.0 copy-done.3
  204.1 0.1 broadcast_bitcast_fusion
  204.2 15.5 %all-to-all-done.3 = bf16[64,8,1024]{2,1,0:T(8,128)(2,1)S(1)} async-done(((bf16[64,8,1024]{2,1,0:T(8,128)(2,1)}), bf16[64,8,1024]{2,1,0:T(8,128)(2,1)S(1)}, u32[]{:S(2)}, u32[]{:S(2)}) %all-to-all-start.3) | async-done | bytes 1048608 | tf_op jit(solution)/shard_map/all_to_all | solution.py:166
  219.7 0.2 convert_reduce_fusion
  219.9 0.6 broadcast_multiply_fusion.1
  (7 shorter events, 0.1 us)
Async XLA Ops:
  0.0 8.2 %copy-start.1 = (s32[8,16]{1,0:T(8,128)S(1)}, s32[8,16]{1,0:T(8,128)}, u32[]{:S(2)}) copy-start(s32[8,16]{1,0:T(8,128)} %param.6) | copy-start | bytes 1540
  0.0 70.0 %all-to-all-start = ((bf16[16,8,128,128]{3,2,1,0:T(8,128)(2,1)}), bf16[16,8,128,128]{3,2,1,0:T(8,128)(2,1)}, u32[]{:S(2)}, u32[]{:S(2)}) async-start(bf16[16,8,128,128]{3,2,1,0:T(8,128)(2,1)} %bitcast.31), calls=%async_computation | async-start | bytes 8388608 | tf_op jit(solution)/shard_map/all_to_all | solution.py:153
  76.3 14.9 %copy-start.2 = (s32[2,4,4]{2,1,0:T(4,128)S(1)}, s32[2,4,4]{2,1,0:T(4,128)}, u32[]{:S(2)}) copy-start(s32[2,4,4]{2,1,0:T(4,128)} %param.8) | copy-start | bytes 388
  76.3 48.6 %all-to-all-start.2 = ((bf16[64,8,2560]{2,1,0:T(8,128)(2,1)}), bf16[64,8,2560]{2,1,0:T(8,128)(2,1)S(1)}, u32[]{:S(2)}, u32[]{:S(2)}) async-start(bf16[64,8,2560]{2,1,0:T(8,128)(2,1)} %bitcast.27), calls=%async_computation.2 | async-start | bytes 5242880 | tf_op jit(solution)/shard_map/all_to_all | solution.py:157
  124.9 5.7 %copy-start = (bf16[64,8,2560]{2,1,0:T(8,128)(2,1)}, bf16[64,8,2560]{2,1,0:T(8,128)(2,1)S(1)}, u32[]{:S(2)}) copy-start(bf16[64,8,2560]{2,1,0:T(8,128)(2,1)S(1)} %all-to-all-done.2) | copy-start | bytes 7864324
  124.9 56.7 %all-to-all-start.1 = ((bf16[64,8,4096]{2,1,0:T(8,128)(2,1)}), bf16[64,8,4096]{2,1,0:T(8,128)(2,1)}, u32[]{:S(2)}, u32[]{:S(2)}) async-start(bf16[64,8,4096]{2,1,0:T(8,128)(2,1)} %bitcast.26), calls=%async_computation.1 | async-start | bytes 8388608 | tf_op jit(solution)/shard_map/all_to_all | solution.py:162
  130.6 51.0 %collective-permute-start = (bf16[512,2560]{1,0:T(8,128)(2,1)S(1)}, bf16[512,2560]{1,0:T(8,128)(2,1)}, u32[]{:S(2)}, u32[]{:S(2)}) collective-permute-start(bf16[512,2560]{1,0:T(8,128)(2,1)S(1)} %bitcast.28), channel_id=1, source_target_pairs={{0,16},{16,0},{1,17},{17,1},{2,18},{18,2},{3,19},{19,3},{4,20},{20... | collective-permute-start | bytes 7864328 | tf_op jit(solution)/shard_map/ppermute | solution.py:160
  181.6 22.5 %copy-start.3 = (s32[1,8]{1,0:T(1,128)S(1)}, s32[1,8]{1,0:T(1,128)}, u32[]{:S(2)}) copy-start(s32[1,8]{1,0:T(1,128)} %param.9) | copy-start | bytes 100
  192.9 26.7 %all-to-all-start.3 = ((bf16[64,8,1024]{2,1,0:T(8,128)(2,1)}), bf16[64,8,1024]{2,1,0:T(8,128)(2,1)S(1)}, u32[]{:S(2)}, u32[]{:S(2)}) async-start(bf16[64,8,1024]{2,1,0:T(8,128)(2,1)} %bitcast.30), calls=%async_computation.3 | async-start | bytes 2097152 | tf_op jit(solution)/shard_map/all_to_all | solution.py:166

commit v2 on v1

v2 whole, which is shorter than its diff:
```python
import jax
import jax.numpy as jnp
from jax import lax
from jax.experimental import pallas as pl
from jax.experimental.pallas import tpu as pltpu
from jax.sharding import Mesh
from jax.sharding import PartitionSpec as P

B = 128
AB = 128
NBLK = 4
NPAIR = NBLK * NBLK
NBAS = NBLK * B
NNZ = 10
N_ROW = 8
N_COL = 16
AUX = AB // N_COL
NCHIP = 64
SUB = B // NCHIP
SPAN = SUB * B
ROWS = NCHIP * AUX
MIB = 1024 * 1024
SMEM = pl.BlockSpec(memory_space=pltpu.SMEM)
VMEM = pl.BlockSpec(memory_space=pltpu.VMEM)
HBM = pl.BlockSpec(memory_space=pltpu.HBM)


def named_kernel(
    block_pairs_ref, arrived_ref, out_ref, slot_of_ref, blocks, scratch, rows_ref, in_sem, out_sem
):
    row = lax.axis_index(("y", "c")).astype(jnp.int32)
    place = jnp.int32(0)
    for k in range(N_COL):
        slot_of_ref[place] = k
        place = jnp.minimum(place + (block_pairs_ref[row, k] >= 0).astype(jnp.int32), N_COL - 1)
    reads, writes = [], []
    for j in range(NNZ):
        reads.append(
            pltpu.make_async_copy(arrived_ref.at[slot_of_ref[j]], blocks.at[j], in_sem.at[j])
        )
        reads[-1].start()
    for j in range(NNZ):
        reads[j].wait()
        for aux in range(AUX):
            block = blocks[j, aux].astype(jnp.float32)
            for sub in range(SUB):
                scratch[j % 2, sub, pl.ds(aux, NCHIP, stride=AUX), :] = block[
                    sub * NCHIP : (sub + 1) * NCHIP
                ]
        for sub in range(SUB):
            rows_ref[:, j * SPAN + sub * B : j * SPAN + (sub + 1) * B] = scratch[
                j % 2, sub
            ].astype(jnp.bfloat16)
        cols = pl.ds(j * SPAN, SPAN)
        writes.append(
            pltpu.make_async_copy(rows_ref.at[:, cols], out_ref.at[:, cols], out_sem.at[j])
        )
        writes[-1].start()
    for copy in writes:
        copy.wait()


def named_slices(block_pairs, arrived):
    return pl.pallas_call(
        named_kernel,
        out_shape=jax.ShapeDtypeStruct((ROWS, NNZ * SPAN), jnp.bfloat16),
        grid_spec=pltpu.PrefetchScalarGridSpec(
            num_scalar_prefetch=1,
            grid=(),
            in_specs=[HBM],
            out_specs=HBM,
            scratch_shapes=[
                pltpu.SMEM((N_COL,), jnp.int32),
                pltpu.VMEM((NNZ, AUX, B, B), jnp.bfloat16),
                pltpu.VMEM((2, SUB, ROWS, B), jnp.float32),
                pltpu.VMEM((ROWS, NNZ * SPAN), jnp.bfloat16),
                pltpu.SemaphoreType.DMA((NNZ,)),
                pltpu.SemaphoreType.DMA((NNZ,)),
            ],
        ),
        compiler_params=pltpu.CompilerParams(vmem_limit_bytes=62 * MIB),
        name="named_slices",
    )(block_pairs, arrived)


def contract_kernel(
    block_pairs_ref,
    mask_ref,
    arrived_ref,
    greens_ref,
    out_ref,
    scratch,
    dense,
    occ_t_ref,
    virt_ref,
    block_slot_ref,
):
    for pair in range(NPAIR):
        block_slot_ref[pair] = -1
    row = lax.axis_index(("y", "c")).astype(jnp.int32)
    for k in range(N_COL):
        pair = block_pairs_ref[row, k]

        @pl.when(pair >= 0)
        def _():
            block_slot_ref[pair] = k

    for m in range(NBLK):
        for n in range(NBLK):
            rows, cols = pl.ds(m * B, B), pl.ds(n * B, B)
            occ = greens_ref[0, rows, cols].astype(jnp.float32)
            occ = jnp.where(mask_ref[m * NBLK + n] > 0, occ, 0.0)
            occ_t_ref[cols, rows] = occ.T.astype(jnp.bfloat16)
            virt = greens_ref[1, rows, cols].astype(jnp.float32)
            virt = jnp.where(mask_ref[NPAIR + m * NBLK + n] > 0, virt, 0.0)
            virt_ref[rows, cols] = virt.astype(jnp.bfloat16)

    def one(aux, carry):
        for m in range(NBLK):
            for n in range(NBLK):
                slot = block_slot_ref[m * NBLK + n]
                block = arrived_ref[jnp.maximum(slot, 0), aux].astype(jnp.float32)
                block = jnp.where(slot >= 0, block, 0.0)
                dense[m * B : (m + 1) * B, n * B : (n + 1) * B] = block.astype(jnp.bfloat16)
        half = jnp.dot(
            occ_t_ref[...], dense[...], preferred_element_type=jnp.float32
        ).astype(jnp.bfloat16)
        full = jnp.dot(half, virt_ref[...], preferred_element_type=jnp.float32)
        for m in range(NBLK):
            for sub in range(SUB):
                row = m * B + sub * NCHIP
                for n in range(NBLK):
                    scratch[(m * NBLK + n) * SUB + sub, pl.ds(aux, NCHIP, stride=AUX), :] = full[
                        row : row + NCHIP, n * B : (n + 1) * B
                    ]
        return carry

    lax.fori_loop(0, AUX, one, 0)
    for k in range(NPAIR * SUB):
        out_ref[:, k * B : (k + 1) * B] = scratch[k].astype(jnp.bfloat16)


def contracted_slices(block_pairs, mask, arrived, greens):
    return pl.pallas_call(
        contract_kernel,
        out_shape=jax.ShapeDtypeStruct((ROWS, NPAIR * SPAN), jnp.bfloat16),
        grid_spec=pltpu.PrefetchScalarGridSpec(
            num_scalar_prefetch=2,
            grid=(),
            in_specs=[VMEM] * 2,
            out_specs=VMEM,
            scratch_shapes=[
                pltpu.VMEM((NPAIR * SUB, ROWS, B), jnp.float32),
                pltpu.VMEM((NBAS, NBAS), jnp.bfloat16),
                pltpu.VMEM((NBAS, NBAS), jnp.bfloat16),
                pltpu.VMEM((NBAS, NBAS), jnp.bfloat16),
                pltpu.SMEM((NPAIR,), jnp.int32),
            ],
        ),
        compiler_params=pltpu.CompilerParams(vmem_limit_bytes=24 * MIB),
        name="contracted_slices",
    )(block_pairs, mask, arrived, greens)


def dense_kernel(block_pairs_ref, own_ref, other_ref, out_ref):
    core = lax.axis_index("c").astype(jnp.int32)

    def one(y, carry):
        rows = pl.ds(pl.multiple_of(y * AB, AB), AB)
        for ref, side in ((own_ref, core), (other_ref, 1 - core)):
            row = 2 * y + side
            cols = pl.ds(pl.multiple_of(row * AB, AB), AB)
            out_ref[:, cols] = jnp.zeros((NPAIR * SPAN, AB), jnp.bfloat16)

            def one_slot(k, place):
                pair = block_pairs_ref[row, k]

                @pl.when(pair >= 0)
                def _():
                    start = pl.multiple_of(pair * SPAN, SPAN)
                    from_ = pl.multiple_of(jnp.minimum(place, NNZ - 1) * SPAN, SPAN)
                    block = ref[rows, pl.ds(from_, SPAN)].astype(jnp.float32)
                    out_ref[pl.ds(start, SPAN), cols] = block.T.astype(jnp.bfloat16)

                return place + (pair >= 0).astype(jnp.int32)

            lax.fori_loop(0, N_COL, one_slot, jnp.int32(0))
        return carry

    lax.fori_loop(0, N_ROW // 2, one, 0)


def dense_named(block_pairs, own, other):
    return pl.pallas_call(
        dense_kernel,
        out_shape=jax.ShapeDtypeStruct((NPAIR * SPAN, N_ROW * AB), jnp.bfloat16),
        grid_spec=pltpu.PrefetchScalarGridSpec(
            num_scalar_prefetch=1,
            grid=(),
            in_specs=[VMEM] * 2,
            out_specs=VMEM,
        ),
        compiler_params=pltpu.CompilerParams(vmem_limit_bytes=18 * MIB),
        cost_estimate=pl.CostEstimate(flops=0, bytes_accessed=14 * MIB, transcendentals=0),
        name="dense_named",
    )(block_pairs, own, other)


STEPS = 4
PART = NPAIR * SPAN // STEPS
QCOLS = 256


def chi_kernel(image_hbm, dense_hbm, out_ref, image, dense, total, image_sem, dense_sem):
    copies = []
    for i in range(STEPS):
        part = pl.ds(i * PART, PART)
        copies.append(
            (
                pltpu.make_async_copy(image_hbm.at[:, part], image.at[:, part], image_sem.at[i]),
                pltpu.make_async_copy(dense_hbm.at[part], dense.at[part], dense_sem.at[i]),
            )
        )
    for pair in copies:
        for copy in pair:
            copy.start()
    for i in range(STEPS):
        for copy in copies[i]:
            copy.wait()
        for q in range(0, N_ROW * AB, QCOLS):
            term = jnp.dot(
                image[:, i * PART : (i + 1) * PART],
                dense[i * PART : (i + 1) * PART, q : q + QCOLS],
                preferred_element_type=jnp.float32,
            )
            if i == 0:
                total[:, q : q + QCOLS] = term
            elif i < STEPS - 1:
                total[:, q : q + QCOLS] += term
            else:
                out_ref[:, q : q + QCOLS] = (total[:, q : q + QCOLS] + term).astype(jnp.bfloat16)


def chi_partials(image, dense):
    return pl.pallas_call(
        chi_kernel,
        out_shape=jax.ShapeDtypeStruct((ROWS, N_ROW * AB), jnp.bfloat16),
        in_specs=[HBM, HBM],
        out_specs=VMEM,
        scratch_shapes=[
            pltpu.VMEM((ROWS, NPAIR * SPAN), jnp.bfloat16),
            pltpu.VMEM((NPAIR * SPAN, N_ROW * AB), jnp.bfloat16),
            pltpu.VMEM((ROWS, N_ROW * AB), jnp.float32),
            pltpu.SemaphoreType.DMA((STEPS,)),
            pltpu.SemaphoreType.DMA((STEPS,)),
        ],
        compiler_params=pltpu.CompilerParams(vmem_limit_bytes=58 * MIB),
        name="chi_partials",
    )(image, dense)


def on_device(x_slots, block_pairs, greens, green_mask, chi_mask):
    chips = ("y", "x", "z")
    arrived = lax.all_to_all(
        x_slots[0, 0].reshape(N_COL, AUX, B, B), ("x", "z"), 0, 0, tiled=True
    )
    own = named_slices(block_pairs, arrived)
    own = lax.all_to_all(
        own.reshape(NCHIP, AUX, NNZ * SPAN), chips, 0, 0, tiled=True
    ).reshape(ROWS, NNZ * SPAN)
    other = lax.ppermute(own, "c", [(0, 1), (1, 0)])
    image = contracted_slices(block_pairs, green_mask.reshape(2 * NPAIR), arrived, greens)
    image = lax.all_to_all(
        image.reshape(NCHIP, AUX, NPAIR * SPAN), chips, 0, 0, tiled=True
    ).reshape(ROWS, NPAIR * SPAN)
    dense = dense_named(block_pairs, own, other)
    part = chi_partials(image, dense)
    part = lax.all_to_all(part.reshape(NCHIP, AUX, N_ROW * AB), chips, 0, 0, tiled=True)
    part, chi_mask = lax.optimization_barrier((part, chi_mask))
    chi = jnp.sum(part.astype(jnp.float32), axis=0)
    return chi * jnp.repeat(chi_mask[0], AB).astype(jnp.float32)[None, :]


def solution(mesh):
    split = Mesh(mesh.devices.reshape(4, 2, 4, 4), ("y", "c", "x", "z"))
    row, col = ("y", "c"), ("x", "z")
    placed = (P(row, col, None, None, None), P(), P(), P(), P(row, None))
    return jax.shard_map(
        on_device,
        mesh=split,
        in_specs=placed,
        out_specs=P(row + col, None),
        check_vma=False,
    )
```

time: 221 us -> 195 us (0.88)
  waiting for transfers between devices: 140 us -> 53.1 us
  blocking collectives: 0 us -> 83.8 us
  starting transfers between devices: 40 us -> 13.5 us
  local copies, waits for them, and re-layouts: 4.57 us -> 8.73 us
  other arithmetic: 4.83 us -> 0.8 us
  Pallas kernels: 31.3 us -> 34.3 us
    all_to_all x0 -> x2, blocking collectives: none -> 83.8 us  [the longest x1 58.8 us: on_device(): lax.all_to_all(x_slots[0, 0].reshape(N_COL, AUX, B, B), ('x', 'z'), 0, 0,...]
    all_to_all x2 -> x0, waiting for transfers between devices: 76.5 us -> none  [the longest x1 61 us: on_device(): lax.all_to_all(x_slots[0, 0].reshape(N_COL, AUX, B, B), ('x', 'z'), 0, 0,...]
    all_to_all x1, waiting for transfers between devices: 50.1 us -> 29.3 us  [on_device(): lax.all_to_all(image.reshape(NCHIP, AUX, NPAIR * SPAN), chips, 0, 0, tile...]
    all_to_all x2 -> x0, starting transfers between devices: 19.3 us -> none  [the longest x1 11.2 us: on_device(): lax.all_to_all(part.reshape(NCHIP, AUX, N_ROW * AB), chips, 0, 0, tiled=T...]
    pallas_call x0 -> x1, Pallas kernels: none -> 12.7 us  [dense_named(): pl.pallas_call(dense_kernel, out_shape=jax.ShapeDtypeStruct((NPAIR * SPAN...]
    unnamed x10 -> x14, local copies, waits for them, and re-layouts: 0.96 us -> 8.58 us
    all_to_all x1, starting transfers between devices: 14.9 us -> 7.74 us  [on_device(): lax.all_to_all(own.reshape(NCHIP, AUX, NNZ * SPAN), chips, 0, 0, tiled=True)]
    all_to_all x1, waiting for transfers between devices: 13.1 us -> 19 us  [on_device(): lax.all_to_all(own.reshape(NCHIP, AUX, NNZ * SPAN), chips, 0, 0, tiled=True)]
  transfers between devices with their start and end apart: 5 -> 3, of which waited for: 4 -> 3; matrix products, arithmetic and copies ran while one was open for 4% -> 0% of each run, Pallas kernels for 6% -> 11%
where the time goes in v2:
time: 195 us; the launch traced here: 194 us
  blocking collectives  83.8 us (43%)
  waiting for transfers between devices  53.1 us (27%)
  Pallas kernels  34.3 us (18%)
  starting transfers between devices  13.5 us (7%)
  local copies, waits for them, and re-layouts  8.73 us (4%)
    all_to_all x1, blocking collectives, on_device(): lax.all_to_all(x_slots[0, 0].reshape(N_COL, AUX, B, B), ('x', 'z'), 0, 0,...  58.8 us
    all_to_all x1, waiting for transfers between devices, on_device(): lax.all_to_all(image.reshape(NCHIP, AUX, NPAIR * SPAN), chips, 0, 0, tile...  29.3 us
    all_to_all x1, blocking collectives, on_device(): lax.all_to_all(part.reshape(NCHIP, AUX, N_ROW * AB), chips, 0, 0, tiled=T...  25 us
    all_to_all x1, waiting for transfers between devices, on_device(): lax.all_to_all(own.reshape(NCHIP, AUX, NNZ * SPAN), chips, 0, 0, tiled=True)  19 us
    pallas_call x1, Pallas kernels, dense_named(): pl.pallas_call(dense_kernel, out_shape=jax.ShapeDtypeStruct((NPAIR * SPAN...  12.7 us
    pallas_call x1, Pallas kernels, contracted_slices(): pl.pallas_call(contract_kernel, out_shape=jax.ShapeDtypeStruct((ROWS, NPA...  9.53 us
    unnamed x14, local copies, waits for them, and re-layouts  8.58 us
    all_to_all x1, starting transfers between devices, on_device(): lax.all_to_all(own.reshape(NCHIP, AUX, NNZ * SPAN), chips, 0, 0, tiled=True)  7.74 us
  transfers between devices with their start and end apart: 3, of which 3 were waited for; matrix products, arithmetic and copies ran while one was open for 0% of the time, Pallas kernels for 11%

profile of v2, /device:TPU:0, one launch (start us, length us, event | category | flops | bytes accessed | tf_op | source)
XLA Modules:
  0.0 194.4 jit_solution(5853423070230870962)
XLA Ops:
  0.0 58.8 %all_to_all.20.arrived_ref = bf16[16,8,128,128]{3,2,1,0:T(8,128)(2,1)} all-to-all(bf16[16,8,128,128]{3,2,1,0:T(8,128)(2,1)} %bitcast.14), channel_id=1, replica_groups=mesh['y'=4,'c'=2,'x'=4,'z'=4] {'x','z'}, dimensions={0} | all-to-all | bytes 8388608 | tf_op jit(solution)/shard_map/all_to_all | solution.py:264
  58.8 4.4 %named_slices.1 = bf16[512,2560]{1,0:T(8,128)(2,1)} custom-call(s32[8,16]{1,0:T(8,128)} %block_pairs_ref.5, bf16[16,8,128,128]{3,2,1,0:T(8,128)(2,1)} %all_to_all.20.arrived_ref), custom_call_target="tpu_custom_call" | custom-call | tf_op jit(solution)/shard_map/named_slices/pallas_call | solution.py:64
  63.2 0.0 copy-start.5
  63.2 0.0 copy-start.4
  63.2 7.7 %all-to-all-start.2 = ((bf16[64,8,2560]{2,1,0:T(8,128)(2,1)}), bf16[64,8,2560]{2,1,0:T(8,128)(2,1)S(1)}, u32[]{:S(2)}, u32[]{:S(2)}) async-start(bf16[64,8,2560]{2,1,0:T(8,128)(2,1)} %bitcast.13), calls=%async_computation.2 | async-start | bytes 5242880 | tf_op jit(solution)/shard_map/all_to_all | solution.py:268
  71.0 0.0 copy-done.5
  71.0 0.1 reshape.26.mask_ref
  71.1 0.0 copy-done.4
  71.1 0.0 copy-start
  71.1 2.2 %copy-done = bf16[16,8,128,128]{3,2,1,0:T(8,128)(2,1)S(1)} copy-done((bf16[16,8,128,128]{3,2,1,0:T(8,128)(2,1)S(1)}, bf16[16,8,128,128]{3,2,1,0:T(8,128)(2,1)}, u32[]{:S(2)}) %copy-start) | copy-done | bytes 4194328
  73.3 0.0 copy-start.3
  73.3 1.2 copy-done.3
  74.5 9.5 %contracted_slices.1 = bf16[512,4096]{1,0:T(8,128)(2,1)S(1)} custom-call(s32[8,16]{1,0:T(8,128)S(1)} %copy-done.4, s32[32]{0:T(128)S(1)} %reshape.26.mask_ref, bf16[16,8,128,128]{3,2,1,0:T(8,128)(2,1)S(1)} %copy-done, bf16[2,512,512]{2,1,0:T(8,128)(2,1)S(1)} %copy-done.3), custom_call_target="tpu_custom_call" | custom-call | tf_op jit(solution)/shard_map/contracted_slices/pallas_call | solution.py:144
  84.0 0.0 copy-start.2
  84.0 1.9 copy-done.2
  86.0 19.0 %all-to-all-done.2 = bf16[64,8,2560]{2,1,0:T(8,128)(2,1)S(1)} async-done(((bf16[64,8,2560]{2,1,0:T(8,128)(2,1)}), bf16[64,8,2560]{2,1,0:T(8,128)(2,1)S(1)}, u32[]{:S(2)}, u32[]{:S(2)}) %all-to-all-start.2) | async-done | bytes 2621472 | tf_op jit(solution)/shard_map/all_to_all | solution.py:268
  104.9 5.7 %all-to-all-start.1 = ((bf16[64,8,4096]{2,1,0:T(8,128)(2,1)}), bf16[64,8,4096]{2,1,0:T(8,128)(2,1)}, u32[]{:S(2)}, u32[]{:S(2)}) async-start(bf16[64,8,4096]{2,1,0:T(8,128)(2,1)} %bitcast.10), calls=%async_computation.1 | async-start | bytes 8388608 | tf_op jit(solution)/shard_map/all_to_all | solution.py:273
  110.7 0.1 collective-permute-start
  110.7 4.9 %collective-permute-done.other_ref = bf16[512,2560]{1,0:T(8,128)(2,1)S(1)} collective-permute-done((bf16[512,2560]{1,0:T(8,128)(2,1)S(1)}, bf16[512,2560]{1,0:T(8,128)(2,1)S(1)}, u32[]{:S(2)}, u32[]{:S(2)}) %collective-permute-start) | collective-permute-done | bytes 2621472 | tf_op jit(solution)/shard_map/ppermute | solution.py:271
  115.6 12.7 %dense_named.1.dense_hbm = bf16[4096,1024]{1,0:T(8,128)(2,1)S(1)} custom-call(s32[8,16]{1,0:T(8,128)S(1)} %copy-done.4, bf16[512,2560]{1,0:T(8,128)(2,1)S(1)} %bitcast.12, bf16[512,2560]{1,0:T(8,128)(2,1)S(1)} %collective-permute-done.other_ref), custom_call_target="tpu_custom_call" | custom-call | bytes 14680064 | tf_op jit(solution)/shard_map/dense_named/pallas_call | solution.py:194
  128.3 0.0 copy-start.1
  128.3 3.2 %copy-done.1 = bf16[4096,1024]{1,0:T(8,128)(2,1)} copy-done((bf16[4096,1024]{1,0:T(8,128)(2,1)}, bf16[4096,1024]{1,0:T(8,128)(2,1)S(1)}, u32[]{:S(2)}) %copy-start.1) | copy-done | bytes 8388632
  131.6 29.3 %all-to-all-done.1 = bf16[64,8,4096]{2,1,0:T(8,128)(2,1)} async-done(((bf16[64,8,4096]{2,1,0:T(8,128)(2,1)}), bf16[64,8,4096]{2,1,0:T(8,128)(2,1)}, u32[]{:S(2)}, u32[]{:S(2)}) %all-to-all-start.1) | async-done | bytes 4194336 | tf_op jit(solution)/shard_map/all_to_all | solution.py:273
  160.8 0.0 copy-start.6
  160.8 7.7 %chi_partials.1 = bf16[512,1024]{1,0:T(8,128)(2,1)} custom-call(bf16[512,4096]{1,0:T(8,128)(2,1)} %bitcast.2.image_hbm, bf16[4096,1024]{1,0:T(8,128)(2,1)} %copy-done.1), custom_call_target="tpu_custom_call" | custom-call | tf_op jit(solution)/shard_map/chi_partials/pallas_call | solution.py:245
  168.5 25.0 %all_to_all.21 = bf16[64,8,1024]{2,1,0:T(8,128)(2,1)S(1)} all-to-all(bf16[64,8,1024]{2,1,0:T(8,128)(2,1)} %bitcast.15), channel_id=1, replica_groups=mesh['y'=4,'c'=2,'x'=4,'z'=4] {'y','x','z'}, dimensions={0} | all-to-all | bytes 2097152 | tf_op jit(solution)/shard_map/all_to_all | solution.py:278
  193.6 0.2 convert_reduce_fusion
  193.7 0.0 copy-done.6
  193.7 0.1 broadcast_bitcast_fusion
  193.8 0.6 broadcast_multiply_fusion
  (1 shorter events, 0.0 us)
Async XLA Ops:
  63.2 7.8 %copy-start.5 = (s32[2,4,4]{2,1,0:T(4,128)S(1)}, s32[2,4,4]{2,1,0:T(4,128)}, u32[]{:S(2)}) copy-start(s32[2,4,4]{2,1,0:T(4,128)} %param.8) | copy-start | bytes 388
  63.2 7.9 %copy-start.4 = (s32[8,16]{1,0:T(8,128)S(1)}, s32[8,16]{1,0:T(8,128)}, u32[]{:S(2)}) copy-start(s32[8,16]{1,0:T(8,128)} %block_pairs_ref.5) | copy-start | bytes 1540
  63.2 41.7 %all-to-all-start.2 = ((bf16[64,8,2560]{2,1,0:T(8,128)(2,1)}), bf16[64,8,2560]{2,1,0:T(8,128)(2,1)S(1)}, u32[]{:S(2)}, u32[]{:S(2)}) async-start(bf16[64,8,2560]{2,1,0:T(8,128)(2,1)} %bitcast.13), calls=%async_computation.2 | async-start | bytes 5242880 | tf_op jit(solution)/shard_map/all_to_all | solution.py:268
  71.1 2.2 %copy-start = (bf16[16,8,128,128]{3,2,1,0:T(8,128)(2,1)S(1)}, bf16[16,8,128,128]{3,2,1,0:T(8,128)(2,1)}, u32[]{:S(2)}) copy-start(bf16[16,8,128,128]{3,2,1,0:T(8,128)(2,1)} %all_to_all.20.arrived_ref) | copy-start | bytes 12582916
  73.3 1.2 copy-start.3
  84.0 1.9 copy-start.2
  104.9 55.9 %all-to-all-start.1 = ((bf16[64,8,4096]{2,1,0:T(8,128)(2,1)}), bf16[64,8,4096]{2,1,0:T(8,128)(2,1)}, u32[]{:S(2)}, u32[]{:S(2)}) async-start(bf16[64,8,4096]{2,1,0:T(8,128)(2,1)} %bitcast.10), calls=%async_computation.1 | async-start | bytes 8388608 | tf_op jit(solution)/shard_map/all_to_all | solution.py:273
  110.7 5.0 %collective-permute-start = (bf16[512,2560]{1,0:T(8,128)(2,1)S(1)}, bf16[512,2560]{1,0:T(8,128)(2,1)S(1)}, u32[]{:S(2)}, u32[]{:S(2)}) collective-permute-start(bf16[512,2560]{1,0:T(8,128)(2,1)S(1)} %bitcast.11), channel_id=1, source_target_pairs={{0,16},{16,0},{1,17},{17,1},{2,18},{18,2},{3,19},{19,3},{4,20},{20... | collective-permute-start | bytes 7864328 | tf_op jit(solution)/shard_map/ppermute | solution.py:271
  128.3 3.2 %copy-start.1 = (bf16[4096,1024]{1,0:T(8,128)(2,1)}, bf16[4096,1024]{1,0:T(8,128)(2,1)S(1)}, u32[]{:S(2)}) copy-start(bf16[4096,1024]{1,0:T(8,128)(2,1)S(1)} %dense_named.1.dense_hbm) | copy-start | bytes 25165828
  160.8 32.9 %copy-start.6 = (s32[1,8]{1,0:T(1,128)S(1)}, s32[1,8]{1,0:T(1,128)}, u32[]{:S(2)}) copy-start(s32[1,8]{1,0:T(1,128)} %param.9) | copy-start | bytes 100

commit v3 on v1

v3 whole, which is shorter than its diff:
```python
import functools

import jax
import jax.numpy as jnp
from jax import lax
from jax.experimental import pallas as pl
from jax.experimental.pallas import tpu as pltpu
from jax.sharding import Mesh
from jax.sharding import PartitionSpec as P

B = 128
AB = 128
NBLK = 4
NPAIR = NBLK * NBLK
NBAS = NBLK * B
NNZ = 10
N_ROW = 8
N_COL = 16
AUX = AB // N_COL
NCHIP = 64
SUB = B // NCHIP
SPAN = SUB * B
ROWS = NCHIP * AUX
NAMED = NNZ * SPAN
WIDTH = NAMED + NPAIR * SPAN
MIB = 1024 * 1024
SMEM = pl.BlockSpec(memory_space=pltpu.SMEM)
VMEM = pl.BlockSpec(memory_space=pltpu.VMEM)


def slices_kernel(
    block_pairs_ref,
    mask_ref,
    arrived_ref,
    greens_ref,
    out_ref,
    pairs_ref,
    slot_of_ref,
    block_slot_ref,
    scratch,
    dense0,
    dense1,
    occ_t_ref,
    virt_ref,
):
    row = lax.axis_index(("y", "c")).astype(jnp.int32)
    for pair in range(NPAIR):
        block_slot_ref[pair] = -1
    place = jnp.int32(0)
    for k in range(N_COL):
        pair = block_pairs_ref[row, k]
        slot_of_ref[place] = k
        place = jnp.minimum(place + (pair >= 0).astype(jnp.int32), N_COL - 1)

        @pl.when(pair >= 0)
        def _():
            block_slot_ref[pair] = k

    for m in range(NBLK):
        for n in range(NBLK):
            rows, cols = pl.ds(m * B, B), pl.ds(n * B, B)
            occ = greens_ref[0, rows, cols].astype(jnp.float32)
            occ = jnp.where(mask_ref[0, m, n] > 0, occ, 0.0)
            occ_t_ref[cols, rows] = occ.T.astype(jnp.bfloat16)
            virt = greens_ref[1, rows, cols].astype(jnp.float32)
            virt = jnp.where(mask_ref[1, m, n] > 0, virt, 0.0)
            virt_ref[rows, cols] = virt.astype(jnp.bfloat16)

    def two(i, carry):
        for u, dense in enumerate((dense0, dense1)):
            aux = 2 * i + u
            for m in range(NBLK):
                for n in range(NBLK):
                    slot = block_slot_ref[m * NBLK + n]
                    block = arrived_ref[jnp.maximum(slot, 0), aux]
                    dense[m * B : (m + 1) * B, n * B : (n + 1) * B] = jnp.where(
                        slot >= 0, block, jnp.zeros_like(block)
                    )
            half = jnp.dot(
                occ_t_ref[...], dense[...], preferred_element_type=jnp.float32
            ).astype(jnp.bfloat16)
            for j in range(NNZ):
                block = arrived_ref[slot_of_ref[j], aux].astype(jnp.float32)
                for sub in range(SUB):
                    scratch[j * SUB + sub, pl.ds(aux, NCHIP, stride=AUX), :] = block[
                        sub * NCHIP : (sub + 1) * NCHIP
                    ]
            full = jnp.dot(half, virt_ref[...], preferred_element_type=jnp.float32)
            for m in range(NBLK):
                for sub in range(SUB):
                    at = m * B + sub * NCHIP
                    for n in range(NBLK):
                        k = (NNZ + m * NBLK + n) * SUB + sub
                        scratch[k, pl.ds(aux, NCHIP, stride=AUX), :] = full[
                            at : at + NCHIP, n * B : (n + 1) * B
                        ]
        return carry

    for i in range(AUX // 2):
        two(i, 0)

    def one_row(row, carry):
        def one_slot(k, place):
            pair = block_pairs_ref[row, k]
            pairs_ref[row, place] = jnp.maximum(pair, 0)
            return jnp.minimum(place + (pair >= 0).astype(jnp.int32), N_COL - 1)

        lax.fori_loop(0, N_COL, one_slot, jnp.int32(0))
        return carry

    lax.fori_loop(0, N_ROW, one_row, 0)
    for k in range((NNZ + NPAIR) * SUB):
        out_ref[:, k * B : (k + 1) * B] = scratch[k].astype(jnp.bfloat16)


def slices(block_pairs, mask, arrived, greens):
    return pl.pallas_call(
        slices_kernel,
        out_shape=(
            jax.ShapeDtypeStruct((ROWS, WIDTH), jnp.bfloat16),
            jax.ShapeDtypeStruct((N_ROW, N_COL), jnp.int32),
        ),
        grid_spec=pltpu.PrefetchScalarGridSpec(
            num_scalar_prefetch=2,
            grid=(),
            in_specs=[VMEM] * 2,
            out_specs=(VMEM, SMEM),
            scratch_shapes=[
                pltpu.SMEM((N_COL,), jnp.int32),
                pltpu.SMEM((NPAIR,), jnp.int32),
                pltpu.VMEM(((NNZ + NPAIR) * SUB, ROWS, B), jnp.float32),
                pltpu.VMEM((NBAS, NBAS), jnp.bfloat16),
                pltpu.VMEM((NBAS, NBAS), jnp.bfloat16),
                pltpu.VMEM((NBAS, NBAS), jnp.bfloat16),
                pltpu.VMEM((NBAS, NBAS), jnp.bfloat16),
            ],
        ),
        compiler_params=pltpu.CompilerParams(vmem_limit_bytes=36 * MIB),
        name="slices",
    )(block_pairs, mask, arrived, greens)


def chi_kernel(side_of, pairs_ref, received_ref, named_ref, *refs):
    out_ref, dense0, dense1 = refs[-3:]
    side = side_of(lax.axis_index("c").astype(jnp.int32))
    for h, dense in enumerate((dense0, dense1)):
        dense[...] = jnp.zeros((2 * AB, NPAIR * SPAN), jnp.bfloat16)
        for v in range(2):
            y = 2 * h + v
            for j in range(NNZ):
                start = pl.multiple_of(pairs_ref[2 * y + side, j] * SPAN, SPAN)
                dense[v * AB : (v + 1) * AB, pl.ds(start, SPAN)] = named_ref[
                    y * AB : (y + 1) * AB, j * SPAN : (j + 1) * SPAN
                ]
        part = lax.dot_general(
            received_ref[:, NAMED:],
            dense[...],
            (((1,), (1,)), ((), ())),
            preferred_element_type=jnp.float32,
        ).astype(jnp.bfloat16)
        for v in range(2):
            row = 2 * (2 * h + v) + side
            out_ref[:, pl.ds(pl.multiple_of(row * AB, AB), AB)] = part[:, v * AB : (v + 1) * AB]


def chi_half(name, side_of, pairs, received, named, *rest):
    return pl.pallas_call(
        functools.partial(chi_kernel, side_of),
        out_shape=jax.ShapeDtypeStruct((ROWS, N_ROW * AB), jnp.bfloat16),
        grid_spec=pltpu.PrefetchScalarGridSpec(
            num_scalar_prefetch=1,
            grid=(),
            in_specs=[VMEM] * (2 + len(rest)),
            out_specs=VMEM,
            scratch_shapes=[pltpu.VMEM((2 * AB, NPAIR * SPAN), jnp.bfloat16)] * 2,
        ),
        input_output_aliases={3: 0} if rest else {},
        cost_estimate=pl.CostEstimate(
            flops=ROWS * N_ROW * AB * NPAIR * SPAN, bytes_accessed=8 * MIB, transcendentals=0
        ),
        compiler_params=pltpu.CompilerParams(vmem_limit_bytes=16 * MIB),
        name=name,
    )(pairs, received, named, *rest)


def on_device(x_slots, block_pairs, greens, green_mask, chi_mask):
    chips = ("y", "x", "z")
    arrived = lax.all_to_all(
        x_slots[0, 0].reshape(N_COL, AUX, B, B), ("x", "z"), 0, 0, tiled=True
    )
    sent, pairs = slices(block_pairs, green_mask, arrived, greens)
    received = lax.all_to_all(sent.reshape(NCHIP, AUX, WIDTH), chips, 0, 0, tiled=True)
    received = received.reshape(ROWS, WIDTH)
    own = received[:, :NAMED]
    other = lax.ppermute(own, "c", [(0, 1), (1, 0)])
    part = chi_half("chi_own", lambda core: core, pairs, received, own)
    part = chi_half("chi_other", lambda core: 1 - core, pairs, received, other, part)
    part = lax.all_to_all(part.reshape(NCHIP, AUX, N_ROW * AB), chips, 0, 0, tiled=True)
    part, chi_mask = lax.optimization_barrier((part, chi_mask))
    chi = jnp.sum(part.astype(jnp.float32), axis=0)
    return chi * jnp.repeat(chi_mask[0], AB).astype(jnp.float32)[None, :]


def solution(mesh):
    split = Mesh(mesh.devices.reshape(4, 2, 4, 4), ("y", "c", "x", "z"))
    row, col = ("y", "c"), ("x", "z")
    placed = (P(row, col, None, None, None), P(), P(), P(), P(row, None))
    return jax.shard_map(
        on_device,
        mesh=split,
        in_specs=placed,
        out_specs=P(row + col, None),
        check_vma=False,
    )
```

time: 221 us -> 190 us (0.86)
  blocking collectives: 0 us -> 170 us
  waiting for transfers between devices: 140 us -> 1.35 us
  starting transfers between devices: 40 us -> 0.27 us
  Pallas kernels: 31.3 us -> 17.8 us
  local copies, waits for them, and re-layouts: 4.57 us -> 0.26 us
  other arithmetic: 4.83 us -> 0.8 us
    all_to_all x0 -> x3, blocking collectives: none -> 170 us  [the longest x1 87.1 us: on_device(): lax.all_to_all(sent.reshape(NCHIP, AUX, WIDTH), chips, 0, 0, tiled=True)]
    all_to_all x4 -> x0, waiting for transfers between devices: 140 us -> none  [the longest x1 61 us: on_device(): lax.all_to_all(x_slots[0, 0].reshape(N_COL, AUX, B, B), ('x', 'z'), 0, 0,...]
    all_to_all x4 -> x0, starting transfers between devices: 39.9 us -> none  [the longest x1 14.9 us: on_device(): lax.all_to_all(own.reshape(NCHIP, AUX, NNZ * SPAN), chips, 0, 0, tiled=True)]
    pallas_call x3, Pallas kernels: 31.3 us -> 17.8 us  [the longest x1 10.8 us: slices(): pl.pallas_call(slices_kernel, out_shape=(jax.ShapeDtypeStruct((ROWS, WIDT...]
  transfers between devices with their start and end apart: 5 -> 1, of which waited for: 4 -> 1; matrix products, arithmetic and copies ran while one was open for 4% -> 0% of each run, Pallas kernels for 6% -> 2%
where the time goes in v3:
time: 190 us
  blocking collectives  170 us (89%)
  Pallas kernels  17.8 us (9%)
    all_to_all x1, blocking collectives, on_device(): lax.all_to_all(sent.reshape(NCHIP, AUX, WIDTH), chips, 0, 0, tiled=True)  87.1 us
    all_to_all x1, blocking collectives, on_device(): lax.all_to_all(x_slots[0, 0].reshape(N_COL, AUX, B, B), ('x', 'z'), 0, 0,...  58.9 us
    all_to_all x1, blocking collectives, on_device(): lax.all_to_all(part.reshape(NCHIP, AUX, N_ROW * AB), chips, 0, 0, tiled=T...  23.6 us
    pallas_call x1, Pallas kernels, slices(): pl.pallas_call(slices_kernel, out_shape=(jax.ShapeDtypeStruct((ROWS, WIDT...  10.8 us
    pallas_call x2, Pallas kernels, chi_half(): pl.pallas_call(functools.partial(chi_kernel, side_of), out_shape=jax.Shap...  7.03 us
  transfers between devices with their start and end apart: 1, of which 1 were waited for; matrix products, arithmetic and copies ran while one was open for 0% of the time, Pallas kernels for 2%

profile of v3, /device:TPU:0, one launch (start us, length us, event | category | flops | bytes accessed | tf_op | source)
XLA Modules:
  0.0 190.1 jit_solution(760727521966509254)
XLA Ops:
  0.0 0.0 copy-start
  0.0 0.0 copy-start.1
  0.0 0.0 copy-start.2
  0.0 58.9 %all_to_all.15.arrived_ref = bf16[16,8,128,128]{3,2,1,0:T(8,128)(2,1)S(1)} all-to-all(bf16[16,8,128,128]{3,2,1,0:T(8,128)(2,1)} %bitcast.13), channel_id=1, replica_groups=mesh['y'=4,'c'=2,'x'=4,'z'=4] {'x','z'}, dimensions={0} | all-to-all | bytes 8388608 | tf_op jit(solution)/shard_map/all_to_all | solution.py:188
  58.9 0.0 copy-done
  58.9 0.0 copy-done.1
  58.9 0.0 copy-done.2
  58.9 10.8 %slices.1 = (bf16[512,6656]{1,0:T(8,128)(2,1)S(1)}, s32[8,16]{1,0:T(8,128)S(1)}) custom-call(s32[8,16]{1,0:T(8,128)S(1)} %copy-done.1, s32[2,4,4]{2,1,0:T(4,128)S(1)} %copy-done.2, bf16[16,8,128,128]{3,2,1,0:T(8,128)(2,1)S(1)} %all_to_all.15.arrived_ref, bf16[2,512,512]{2,1,0:T(8,128)(2,1)S(1)} %copy-done), custom_call_target="tpu_custom_call" | custom-call | tf_op jit(solution)/shard_map/slices/pallas_call | solution.py:117
  69.7 87.1 %all_to_all.16 = bf16[64,8,6656]{2,1,0:T(8,128)(2,1)S(1)} all-to-all(bf16[64,8,6656]{2,1,0:T(8,128)(2,1)S(1)} %bitcast.12), channel_id=1, replica_groups=mesh['y'=4,'c'=2,'x'=4,'z'=4] {'y','x','z'}, dimensions={0} | all-to-all | bytes 13631488 | tf_op jit(solution)/shard_map/all_to_all | solution.py:192
  156.7 0.2 slice.4.named_ref
  156.9 0.3 collective-permute-start
  157.2 3.5 %chi_own.1.refs_0_ = bf16[512,1024]{1,0:T(8,128)(2,1)S(1)} custom-call(s32[8,16]{1,0:T(8,128)S(1)} %get-tuple-element.9.pairs_ref, bf16[512,6656]{1,0:T(8,128)(2,1)S(1)} %bitcast.9, bf16[512,2560]{1,0:T(8,128)(2,1)S(1)} %slice.4.named_ref), custom_call_target="tpu_custom_call" | custom-call | flops 2147483648 | bytes 8388608 | tf_op jit(solution)/shard_map/chi_own/pallas_call | solution.py:167
  160.7 0.0 copy-start.3
  160.7 1.4 collective-permute-done.named_ref
  162.1 3.5 %chi_other.1 = bf16[512,1024]{1,0:T(8,128)(2,1)S(1)} custom-call(s32[8,16]{1,0:T(8,128)S(1)} %get-tuple-element.9.pairs_ref, bf16[512,6656]{1,0:T(8,128)(2,1)S(1)} %bitcast.10, bf16[512,2560]{1,0:T(8,128)(2,1)S(1)} %collective-permute-done.named_ref, bf16[512,1024]{1,0:T(8,128)(2,1)S(1)} %chi_own.1.refs_0_), custom_call_target="tpu_custom_call", output_to_operand_aliasing={{}: (3, {})} | custom-call | flops 2147483648 | bytes 8388608 | tf_op jit(solution)/shard_map/chi_other/pallas_call | solution.py:167
  165.6 23.6 %all_to_all.17 = bf16[64,8,1024]{2,1,0:T(8,128)(2,1)S(1)} all-to-all(bf16[64,8,1024]{2,1,0:T(8,128)(2,1)S(1)} %bitcast.11), channel_id=1, replica_groups=mesh['y'=4,'c'=2,'x'=4,'z'=4] {'y','x','z'}, dimensions={0} | all-to-all | bytes 2097152 | tf_op jit(solution)/shard_map/all_to_all | solution.py:198
  189.2 0.2 convert_reduce_fusion
  189.4 0.0 copy-done.3
  189.4 0.1 broadcast_bitcast_fusion
  189.5 0.6 broadcast_multiply_fusion
  (1 shorter events, 0.0 us)
Async XLA Ops:
  0.0 58.9 %copy-start = (bf16[2,512,512]{2,1,0:T(8,128)(2,1)S(1)}, bf16[2,512,512]{2,1,0:T(8,128)(2,1)}, u32[]{:S(2)}) copy-start(bf16[2,512,512]{2,1,0:T(8,128)(2,1)} %greens_ref.1) | copy-start | bytes 3145732
  0.0 58.9 %copy-start.1 = (s32[8,16]{1,0:T(8,128)S(1)}, s32[8,16]{1,0:T(8,128)}, u32[]{:S(2)}) copy-start(s32[8,16]{1,0:T(8,128)} %block_pairs_ref.1) | copy-start | bytes 1540
  0.0 58.9 %copy-start.2 = (s32[2,4,4]{2,1,0:T(4,128)S(1)}, s32[2,4,4]{2,1,0:T(4,128)}, u32[]{:S(2)}) copy-start(s32[2,4,4]{2,1,0:T(4,128)} %mask_ref.1) | copy-start | bytes 388
  156.9 5.2 %collective-permute-start = (bf16[512,2560]{1,0:T(8,128)(2,1)S(1)}, bf16[512,2560]{1,0:T(8,128)(2,1)S(1)}, u32[]{:S(2)}, u32[]{:S(2)}) collective-permute-start(bf16[512,2560]{1,0:T(8,128)(2,1)S(1)} %slice.4.named_ref), channel_id=1, source_target_pairs={{0,16},{16,0},{1,17},{17,1},{2,18},{18,2},{3,19},{19,3},{4,20},{20... | collective-permute-start | bytes 7864328 | tf_op jit(solution)/shard_map/ppermute | solution.py:195
  160.7 28.7 %copy-start.3 = (s32[1,8]{1,0:T(1,128)S(1)}, s32[1,8]{1,0:T(1,128)}, u32[]{:S(2)}) copy-start(s32[1,8]{1,0:T(1,128)} %param.9) | copy-start | bytes 100

commit v4 on v3

v4 whole, which is shorter than its diff:
```python
import jax
import jax.numpy as jnp
from jax import lax
from jax.experimental import pallas as pl
from jax.experimental.pallas import tpu as pltpu
from jax.sharding import Mesh
from jax.sharding import PartitionSpec as P

B = 128
AB = 128
NBLK = 4
NPAIR = NBLK * NBLK
NBAS = NBLK * B
NNZ = 10
N_ROW = 8
N_COL = 16
AUX = AB // N_COL
NCHIP = 64
SUB = B // NCHIP
SPAN = SUB * B
ROWS = NCHIP * AUX
NAMED = NNZ * SPAN
WIDTH = NAMED + NPAIR * SPAN
MIB = 1024 * 1024
SMEM = pl.BlockSpec(memory_space=pltpu.SMEM)
VMEM = pl.BlockSpec(memory_space=pltpu.VMEM)


def slices_kernel(
    block_pairs_ref,
    mask_ref,
    arrived_ref,
    greens_ref,
    out_ref,
    slot_of_ref,
    block_slot_ref,
    scratch,
    half_scratch,
    dense0,
    dense1,
    occ_t_ref,
    virt_ref,
):
    row = lax.axis_index(("y", "c")).astype(jnp.int32)
    for pair in range(NPAIR):
        block_slot_ref[pair] = -1
    place = jnp.int32(0)
    for k in range(N_COL):
        pair = block_pairs_ref[row, k]
        slot_of_ref[place] = k
        place = jnp.minimum(place + (pair >= 0).astype(jnp.int32), N_COL - 1)

        @pl.when(pair >= 0)
        def _():
            block_slot_ref[pair] = k

    for m in range(NBLK):
        for n in range(NBLK):
            rows, cols = pl.ds(m * B, B), pl.ds(n * B, B)
            occ = greens_ref[0, rows, cols].astype(jnp.float32)
            occ = jnp.where(mask_ref[0, m, n] > 0, occ, 0.0)
            occ_t_ref[cols, rows] = occ.T.astype(jnp.bfloat16)
            virt = greens_ref[1, rows, cols].astype(jnp.float32)
            virt = jnp.where(mask_ref[1, m, n] > 0, virt, 0.0)
            virt_ref[rows, cols] = virt.astype(jnp.bfloat16)

    def named_rows(aux):
        for j in range(NNZ):
            block = arrived_ref[slot_of_ref[j], aux].astype(jnp.float32)
            for sub in range(SUB):
                scratch[j * SUB + sub, pl.ds(aux, NCHIP, stride=AUX), :] = block[
                    sub * NCHIP : (sub + 1) * NCHIP
                ]

    for aux in range(AUX):
        dense = dense0 if aux % 2 == 0 else dense1
        for m in range(NBLK):
            for n in range(NBLK):
                slot = block_slot_ref[m * NBLK + n]
                block = arrived_ref[jnp.maximum(slot, 0), aux]
                dense[m * B : (m + 1) * B, n * B : (n + 1) * B] = jnp.where(
                    slot >= 0, block, jnp.zeros_like(block)
                )
        half = jnp.dot(occ_t_ref[...], dense[...], preferred_element_type=jnp.float32)
        named_rows(aux)
        for m in range(NBLK):
            for sub in range(SUB):
                at = m * B + sub * NCHIP
                for n in range(NBLK):
                    half_scratch[
                        (m * SUB + sub) * NBLK + n, pl.ds(aux, NCHIP, stride=AUX), :
                    ] = half[at : at + NCHIP, n * B : (n + 1) * B]
    for m in range(NBLK):
        for sub in range(SUB):
            at = (m * SUB + sub) * NBLK
            half = jnp.concatenate(
                [half_scratch[at + n].astype(jnp.bfloat16) for n in range(NBLK)], axis=1
            )
            full = jnp.dot(half, virt_ref[...], preferred_element_type=jnp.float32)
            for n in range(NBLK):
                k = (NNZ + m * NBLK + n) * SUB + sub
                out_ref[:, k * B : (k + 1) * B] = full[:, n * B : (n + 1) * B].astype(
                    jnp.bfloat16
                )
            for k in range(m * SUB + sub, NNZ * SUB, NBLK * SUB):
                out_ref[:, k * B : (k + 1) * B] = scratch[k].astype(jnp.bfloat16)


def slices(block_pairs, mask, arrived, greens):
    return pl.pallas_call(
        slices_kernel,
        out_shape=jax.ShapeDtypeStruct((ROWS, WIDTH), jnp.bfloat16),
        grid_spec=pltpu.PrefetchScalarGridSpec(
            num_scalar_prefetch=2,
            grid=(),
            in_specs=[VMEM] * 2,
            out_specs=VMEM,
            scratch_shapes=[
                pltpu.SMEM((N_COL,), jnp.int32),
                pltpu.SMEM((NPAIR,), jnp.int32),
                pltpu.VMEM((NNZ * SUB, ROWS, B), jnp.float32),
                pltpu.VMEM((NBLK * SUB * NBLK, ROWS, B), jnp.float32),
                pltpu.VMEM((NBAS, NBAS), jnp.bfloat16),
                pltpu.VMEM((NBAS, NBAS), jnp.bfloat16),
                pltpu.VMEM((NBAS, NBAS), jnp.bfloat16),
                pltpu.VMEM((NBAS, NBAS), jnp.bfloat16),
            ],
        ),
        compiler_params=pltpu.CompilerParams(vmem_limit_bytes=36 * MIB),
        name="slices",
    )(block_pairs, mask, arrived, greens)


def chi_rows(side, pairs_ref, received_ref, named_ref, out_ref, dense_refs):
    for h, dense in enumerate(dense_refs):
        dense[...] = jnp.zeros((2 * AB, NPAIR * SPAN), jnp.bfloat16)
        for v in range(2):
            y = 2 * h + v
            for j in range(NNZ):
                start = pl.multiple_of(pairs_ref[2 * y + side, j] * SPAN, SPAN)
                dense[v * AB : (v + 1) * AB, pl.ds(start, SPAN)] = named_ref[
                    y * AB : (y + 1) * AB, j * SPAN : (j + 1) * SPAN
                ]
        part = lax.dot_general(
            received_ref[:, NAMED:],
            dense[...],
            (((1,), (1,)), ((), ())),
            preferred_element_type=jnp.float32,
        ).astype(jnp.bfloat16)
        for v in range(2):
            row = 2 * (2 * h + v) + side
            out_ref[:, pl.ds(pl.multiple_of(row * AB, AB), AB)] = part[:, v * AB : (v + 1) * AB]


def own_kernel(block_pairs_ref, received_ref, out_ref, pairs_ref, *dense_refs):
    for row in range(N_ROW):
        place = jnp.int32(0)
        for k in range(N_COL):
            pair = block_pairs_ref[row, k]
            pairs_ref[row, place] = jnp.maximum(pair, 0)
            place = jnp.minimum(place + (pair >= 0).astype(jnp.int32), N_COL - 1)
    core = lax.axis_index("c").astype(jnp.int32)
    chi_rows(core, pairs_ref, received_ref, received_ref, out_ref, dense_refs)


def other_kernel(pairs_ref, received_ref, named_ref, part_ref, out_ref, *dense_refs):
    del part_ref
    core = lax.axis_index("c").astype(jnp.int32)
    chi_rows(1 - core, pairs_ref, received_ref, named_ref, out_ref, dense_refs)


def chi_half(kernel, name, *operands):
    first = len(operands) == 2
    part = jax.ShapeDtypeStruct((ROWS, N_ROW * AB), jnp.bfloat16)
    table = jax.ShapeDtypeStruct((N_ROW, N_COL), jnp.int32)
    return pl.pallas_call(
        kernel,
        out_shape=(part, table) if first else part,
        grid_spec=pltpu.PrefetchScalarGridSpec(
            num_scalar_prefetch=1,
            grid=(),
            in_specs=[VMEM] * (len(operands) - 1),
            out_specs=(VMEM, SMEM) if first else VMEM,
            scratch_shapes=[pltpu.VMEM((2 * AB, NPAIR * SPAN), jnp.bfloat16)] * 2,
        ),
        input_output_aliases={} if first else {3: 0},
        cost_estimate=pl.CostEstimate(
            flops=ROWS * N_ROW * AB * NPAIR * SPAN, bytes_accessed=8 * MIB, transcendentals=0
        ),
        compiler_params=pltpu.CompilerParams(vmem_limit_bytes=16 * MIB),
        name=name,
    )(*operands)


def on_device(x_slots, block_pairs, greens, green_mask, chi_mask):
    chips = ("y", "x", "z")
    arrived = lax.all_to_all(
        x_slots[0, 0].reshape(N_COL, AUX, B, B), ("x", "z"), 0, 0, tiled=True
    )
    sent = slices(block_pairs, green_mask, arrived, greens)
    received = lax.all_to_all(sent.reshape(NCHIP, AUX, WIDTH), chips, 0, 0, tiled=True)
    received = received.reshape(ROWS, WIDTH)
    own = received[:, :NAMED]
    other = lax.ppermute(own, "c", [(0, 1), (1, 0)])
    part, pairs = chi_half(own_kernel, "chi_own", block_pairs, received)
    part = chi_half(other_kernel, "chi_other", pairs, received, other, part)
    part = lax.all_to_all(part.reshape(NCHIP, AUX, N_ROW * AB), chips, 0, 0, tiled=True)
    part, chi_mask = lax.optimization_barrier((part, chi_mask))
    chi = jnp.sum(part.astype(jnp.float32), axis=0)
    return chi * jnp.repeat(chi_mask[0], AB).astype(jnp.float32)[None, :]


def solution(mesh):
    split = Mesh(mesh.devices.reshape(4, 2, 4, 4), ("y", "c", "x", "z"))
    row, col = ("y", "c"), ("x", "z")
    placed = (P(row, col, None, None, None), P(), P(), P(), P(row, None))
    return jax.shard_map(
        on_device,
        mesh=split,
        in_specs=placed,
        out_specs=P(row + col, None),
        check_vma=False,
    )
```

time: 190 us -> 189 us (level)
  no operation moved by 1% of the time
where the time goes in v4:
time: 189 us; the launch traced here: 188 us
  blocking collectives  170 us (90%)
  Pallas kernels  16.3 us (9%)
    all_to_all x1, blocking collectives, on_device(): lax.all_to_all(sent.reshape(NCHIP, AUX, WIDTH), chips, 0, 0, tiled=True)  87.1 us
    all_to_all x1, blocking collectives, on_device(): lax.all_to_all(x_slots[0, 0].reshape(N_COL, AUX, B, B), ('x', 'z'), 0, 0,...  58.9 us
    all_to_all x1, blocking collectives, on_device(): lax.all_to_all(part.reshape(NCHIP, AUX, N_ROW * AB), chips, 0, 0, tiled=T...  23.6 us
    pallas_call x1, Pallas kernels, slices(): pl.pallas_call(slices_kernel, out_shape=jax.ShapeDtypeStruct((ROWS, WIDTH...  9 us
    pallas_call x2, Pallas kernels, chi_half(): pl.pallas_call(kernel, out_shape=(part, table) if first else part, grid_s...  7.31 us
  transfers between devices with their start and end apart: 1, of which 1 were waited for; matrix products, arithmetic and copies ran while one was open for 0% of the time, Pallas kernels for 2%

profile of v4, /device:TPU:0, one launch (start us, length us, event | category | flops | bytes accessed | tf_op | source)
XLA Modules:
  0.0 188.4 jit_solution(11249116100835747144)
XLA Ops:
  0.0 0.0 copy-start
  0.0 0.0 copy-start.1
  0.0 0.0 copy-start.2
  0.0 58.9 %all_to_all.15.arrived_ref = bf16[16,8,128,128]{3,2,1,0:T(8,128)(2,1)S(1)} all-to-all(bf16[16,8,128,128]{3,2,1,0:T(8,128)(2,1)} %bitcast.13), channel_id=1, replica_groups=mesh['y'=4,'c'=2,'x'=4,'z'=4] {'x','z'}, dimensions={0} | all-to-all | bytes 8388608 | tf_op jit(solution)/shard_map/all_to_all | solution.py:197
  58.9 0.0 copy-done
  58.9 0.0 copy-done.1
  58.9 0.0 copy-done.2
  58.9 9.0 %slices.1 = bf16[512,6656]{1,0:T(8,128)(2,1)S(1)} custom-call(s32[8,16]{1,0:T(8,128)S(1)} %copy-done.2, s32[2,4,4]{2,1,0:T(4,128)S(1)} %copy-done.1, bf16[16,8,128,128]{3,2,1,0:T(8,128)(2,1)S(1)} %all_to_all.15.arrived_ref, bf16[2,512,512]{2,1,0:T(8,128)(2,1)S(1)} %copy-done), custom_call_target="tpu_custom_call" | custom-call | tf_op jit(solution)/shard_map/slices/pallas_call | solution.py:110
  67.9 87.1 %all_to_all.16 = bf16[64,8,6656]{2,1,0:T(8,128)(2,1)S(1)} all-to-all(bf16[64,8,6656]{2,1,0:T(8,128)(2,1)S(1)} %bitcast.11), channel_id=1, replica_groups=mesh['y'=4,'c'=2,'x'=4,'z'=4] {'y','x','z'}, dimensions={0} | all-to-all | bytes 13631488 | tf_op jit(solution)/shard_map/all_to_all | solution.py:201
  155.0 0.2 slice.4
  155.1 0.3 collective-permute-start
  155.4 3.8 %chi_own.1 = (bf16[512,1024]{1,0:T(8,128)(2,1)S(1)}, s32[8,16]{1,0:T(8,128)S(1)}) custom-call(s32[8,16]{1,0:T(8,128)S(1)} %copy-done.2, bf16[512,6656]{1,0:T(8,128)(2,1)S(1)} %bitcast.9), custom_call_target="tpu_custom_call" | custom-call | flops 2147483648 | bytes 8388608 | tf_op jit(solution)/shard_map/chi_own/pallas_call | solution.py:176
  159.2 1.1 collective-permute-done.named_ref
  160.3 0.0 copy-start.3
  160.3 3.5 %chi_other.1 = bf16[512,1024]{1,0:T(8,128)(2,1)S(1)} custom-call(s32[8,16]{1,0:T(8,128)S(1)} %get-tuple-element.9.pairs_ref, bf16[512,6656]{1,0:T(8,128)(2,1)S(1)} %bitcast.10, bf16[512,2560]{1,0:T(8,128)(2,1)S(1)} %collective-permute-done.named_ref, bf16[512,1024]{1,0:T(8,128)(2,1)S(1)} %get-tuple-element.10.part_ref), custom_call_target="tpu_custom_call", output_to_operand_aliasing={{}: (3, {})} | custom-call | flops 2147483648 | bytes 8388608 | tf_op jit(solution)/shard_map/chi_other/pallas_call | solution.py:176
  163.8 23.6 %all_to_all.17 = bf16[64,8,1024]{2,1,0:T(8,128)(2,1)S(1)} all-to-all(bf16[64,8,1024]{2,1,0:T(8,128)(2,1)S(1)} %bitcast.12), channel_id=1, replica_groups=mesh['y'=4,'c'=2,'x'=4,'z'=4] {'y','x','z'}, dimensions={0} | all-to-all | bytes 2097152 | tf_op jit(solution)/shard_map/all_to_all | solution.py:207
  187.5 0.2 convert_reduce_fusion
  187.6 0.0 copy-done.3
  187.7 0.1 broadcast_bitcast_fusion
  187.7 0.6 broadcast_multiply_fusion
  (1 shorter events, 0.0 us)
Async XLA Ops:
  0.0 58.9 %copy-start = (bf16[2,512,512]{2,1,0:T(8,128)(2,1)S(1)}, bf16[2,512,512]{2,1,0:T(8,128)(2,1)}, u32[]{:S(2)}) copy-start(bf16[2,512,512]{2,1,0:T(8,128)(2,1)} %greens_ref.1) | copy-start | bytes 3145732
  0.0 58.9 %copy-start.1 = (s32[2,4,4]{2,1,0:T(4,128)S(1)}, s32[2,4,4]{2,1,0:T(4,128)}, u32[]{:S(2)}) copy-start(s32[2,4,4]{2,1,0:T(4,128)} %mask_ref.1) | copy-start | bytes 388
  0.0 58.9 %copy-start.2 = (s32[8,16]{1,0:T(8,128)S(1)}, s32[8,16]{1,0:T(8,128)}, u32[]{:S(2)}) copy-start(s32[8,16]{1,0:T(8,128)} %block_pairs_ref.3) | copy-start | bytes 1540
  155.1 5.2 %collective-permute-start = (bf16[512,2560]{1,0:T(8,128)(2,1)S(1)}, bf16[512,2560]{1,0:T(8,128)(2,1)S(1)}, u32[]{:S(2)}, u32[]{:S(2)}) collective-permute-start(bf16[512,2560]{1,0:T(8,128)(2,1)S(1)} %slice.4), channel_id=1, source_target_pairs={{0,16},{16,0},{1,17},{17,1},{2,18},{18,2},{3,19},{19,3},{4,20},{20... | collective-permute-start | bytes 7864328 | tf_op jit(solution)/shard_map/ppermute | solution.py:204
  160.3 27.3 %copy-start.3 = (s32[1,8]{1,0:T(1,128)S(1)}, s32[1,8]{1,0:T(1,128)}, u32[]{:S(2)}) copy-start(s32[1,8]{1,0:T(1,128)} %param.9) | copy-start | bytes 100

commit v5 on v4

--- a/solution.py
+++ b/solution.py
@@ -36,8 +36,6 @@
     block_slot_ref,
     scratch,
     half_scratch,
-    dense0,
-    dense1,
     occ_t_ref,
     virt_ref,
 ):
@@ -73,15 +71,19 @@
                 ]
 
     for aux in range(AUX):
-        dense = dense0 if aux % 2 == 0 else dense1
+        block_rows = []
         for m in range(NBLK):
+            blocks = []
             for n in range(NBLK):
                 slot = block_slot_ref[m * NBLK + n]
                 block = arrived_ref[jnp.maximum(slot, 0), aux]
-                dense[m * B : (m + 1) * B, n * B : (n + 1) * B] = jnp.where(
-                    slot >= 0, block, jnp.zeros_like(block)
-                )
-        half = jnp.dot(occ_t_ref[...], dense[...], preferred_element_type=jnp.float32)
+                blocks.append(jnp.where(slot >= 0, block, jnp.zeros_like(block)))
+            block_rows.append(jnp.concatenate(blocks, axis=1))
+        half = jnp.dot(
+            occ_t_ref[...],
+            jnp.concatenate(block_rows, axis=0),
+            preferred_element_type=jnp.float32,
+        )
         named_rows(aux)
         for m in range(NBLK):
             for sub in range(SUB):
@@ -122,8 +124,6 @@
                 pltpu.VMEM((NBLK * SUB * NBLK, ROWS, B), jnp.float32),
                 pltpu.VMEM((NBAS, NBAS), jnp.bfloat16),
                 pltpu.VMEM((NBAS, NBAS), jnp.bfloat16),
-                pltpu.VMEM((NBAS, NBAS), jnp.bfloat16),
-                pltpu.VMEM((NBAS, NBAS), jnp.bfloat16),
             ],
         ),
         compiler_params=pltpu.CompilerParams(vmem_limit_bytes=36 * MIB),

time: 189 us -> 188 us (level)
  no operation moved by 1% of the time
where the time goes in v5:
time: 188 us
  blocking collectives  170 us (90%)
  Pallas kernels  15.8 us (8%)
    all_to_all x1, blocking collectives, on_device(): lax.all_to_all(sent.reshape(NCHIP, AUX, WIDTH), chips, 0, 0, tiled=True)  87.1 us
    all_to_all x1, blocking collectives, on_device(): lax.all_to_all(x_slots[0, 0].reshape(N_COL, AUX, B, B), ('x', 'z'), 0, 0,...  58.9 us
    all_to_all x1, blocking collectives, on_device(): lax.all_to_all(part.reshape(NCHIP, AUX, N_ROW * AB), chips, 0, 0, tiled=T...  23.7 us
    pallas_call x1, Pallas kernels, slices(): pl.pallas_call(slices_kernel, out_shape=jax.ShapeDtypeStruct((ROWS, WIDTH...  8.51 us
    pallas_call x2, Pallas kernels, chi_half(): pl.pallas_call(kernel, out_shape=(part, table) if first else part, grid_s...  7.31 us
  transfers between devices with their start and end apart: 1, of which 1 were waited for; matrix products, arithmetic and copies ran while one was open for 0% of the time, Pallas kernels for 2%

profile of v5, /device:TPU:0, one launch (start us, length us, event | category | flops | bytes accessed | tf_op | source)
XLA Modules:
  0.0 187.7 jit_solution(6207030850739496048)
XLA Ops:
  0.0 0.0 copy-start
  0.0 0.0 copy-start.1
  0.0 0.0 copy-start.2
  0.0 58.9 %all_to_all.15.arrived_ref = bf16[16,8,128,128]{3,2,1,0:T(8,128)(2,1)S(1)} all-to-all(bf16[16,8,128,128]{3,2,1,0:T(8,128)(2,1)} %bitcast.13), channel_id=1, replica_groups=mesh['y'=4,'c'=2,'x'=4,'z'=4] {'x','z'}, dimensions={0} | all-to-all | bytes 8388608 | tf_op jit(solution)/shard_map/all_to_all | solution.py:197
  58.9 0.0 copy-done
  58.9 0.0 copy-done.1
  58.9 0.0 copy-done.2
  58.9 8.5 %slices.1 = bf16[512,6656]{1,0:T(8,128)(2,1)S(1)} custom-call(s32[8,16]{1,0:T(8,128)S(1)} %copy-done.2, s32[2,4,4]{2,1,0:T(4,128)S(1)} %copy-done.1, bf16[16,8,128,128]{3,2,1,0:T(8,128)(2,1)S(1)} %all_to_all.15.arrived_ref, bf16[2,512,512]{2,1,0:T(8,128)(2,1)S(1)} %copy-done), custom_call_target="tpu_custom_call" | custom-call | tf_op jit(solution)/shard_map/slices/pallas_call | solution.py:112
  67.4 87.1 %all_to_all.16 = bf16[64,8,6656]{2,1,0:T(8,128)(2,1)S(1)} all-to-all(bf16[64,8,6656]{2,1,0:T(8,128)(2,1)S(1)} %bitcast.11), channel_id=1, replica_groups=mesh['y'=4,'c'=2,'x'=4,'z'=4] {'y','x','z'}, dimensions={0} | all-to-all | bytes 13631488 | tf_op jit(solution)/shard_map/all_to_all | solution.py:201
  154.5 0.2 slice.4
  154.7 0.1 collective-permute-start
  154.7 3.8 %chi_own.1 = (bf16[512,1024]{1,0:T(8,128)(2,1)S(1)}, s32[8,16]{1,0:T(8,128)S(1)}) custom-call(s32[8,16]{1,0:T(8,128)S(1)} %copy-done.2, bf16[512,6656]{1,0:T(8,128)(2,1)S(1)} %bitcast.9), custom_call_target="tpu_custom_call" | custom-call | flops 2147483648 | bytes 8388608 | tf_op jit(solution)/shard_map/chi_own/pallas_call | solution.py:176
  158.6 1.1 collective-permute-done.named_ref
  159.6 0.0 copy-start.3
  159.6 3.5 %chi_other.1 = bf16[512,1024]{1,0:T(8,128)(2,1)S(1)} custom-call(s32[8,16]{1,0:T(8,128)S(1)} %get-tuple-element.9.pairs_ref, bf16[512,6656]{1,0:T(8,128)(2,1)S(1)} %bitcast.10, bf16[512,2560]{1,0:T(8,128)(2,1)S(1)} %collective-permute-done.named_ref, bf16[512,1024]{1,0:T(8,128)(2,1)S(1)} %get-tuple-element.10.part_ref), custom_call_target="tpu_custom_call", output_to_operand_aliasing={{}: (3, {})} | custom-call | flops 2147483648 | bytes 8388608 | tf_op jit(solution)/shard_map/chi_other/pallas_call | solution.py:176
  163.2 23.7 %all_to_all.17 = bf16[64,8,1024]{2,1,0:T(8,128)(2,1)S(1)} all-to-all(bf16[64,8,1024]{2,1,0:T(8,128)(2,1)S(1)} %bitcast.12), channel_id=1, replica_groups=mesh['y'=4,'c'=2,'x'=4,'z'=4] {'y','x','z'}, dimensions={0} | all-to-all | bytes 2097152 | tf_op jit(solution)/shard_map/all_to_all | solution.py:207
  186.8 0.2 convert_reduce_fusion
  187.0 0.0 copy-done.3
  187.0 0.1 broadcast_bitcast_fusion
  187.1 0.6 broadcast_multiply_fusion
  (1 shorter events, 0.0 us)
Async XLA Ops:
  0.0 58.9 %copy-start = (bf16[2,512,512]{2,1,0:T(8,128)(2,1)S(1)}, bf16[2,512,512]{2,1,0:T(8,128)(2,1)}, u32[]{:S(2)}) copy-start(bf16[2,512,512]{2,1,0:T(8,128)(2,1)} %greens_ref.1) | copy-start | bytes 3145732
  0.0 58.9 %copy-start.1 = (s32[2,4,4]{2,1,0:T(4,128)S(1)}, s32[2,4,4]{2,1,0:T(4,128)}, u32[]{:S(2)}) copy-start(s32[2,4,4]{2,1,0:T(4,128)} %mask_ref.1) | copy-start | bytes 388
  0.0 58.9 %copy-start.2 = (s32[8,16]{1,0:T(8,128)S(1)}, s32[8,16]{1,0:T(8,128)}, u32[]{:S(2)}) copy-start(s32[8,16]{1,0:T(8,128)} %block_pairs_ref.3) | copy-start | bytes 1540
  154.7 5.0 %collective-permute-start = (bf16[512,2560]{1,0:T(8,128)(2,1)S(1)}, bf16[512,2560]{1,0:T(8,128)(2,1)S(1)}, u32[]{:S(2)}, u32[]{:S(2)}) collective-permute-start(bf16[512,2560]{1,0:T(8,128)(2,1)S(1)} %slice.4), channel_id=1, source_target_pairs={{0,16},{16,0},{1,17},{17,1},{2,18},{18,2},{3,19},{19,3},{4,20},{20... | collective-permute-start | bytes 7864328 | tf_op jit(solution)/shard_map/ppermute | solution.py:204
  159.6 27.3 %copy-start.3 = (s32[1,8]{1,0:T(1,128)S(1)}, s32[1,8]{1,0:T(1,128)}, u32[]{:S(2)}) copy-start(s32[1,8]{1,0:T(1,128)} %param.9) | copy-start | bytes 100

commit v6 on v5

--- a/solution.py
+++ b/solution.py
@@ -131,9 +131,10 @@
     )(block_pairs, mask, arrived, greens)
 
 
-def chi_rows(side, pairs_ref, received_ref, named_ref, out_ref, dense_refs):
+def chi_rows(side, pairs_ref, received_ref, named_ref, out_ref, dense_refs, blank):
     for h, dense in enumerate(dense_refs):
-        dense[...] = jnp.zeros((2 * AB, NPAIR * SPAN), jnp.bfloat16)
+        if blank:
+            dense[...] = jnp.zeros((2 * AB, NPAIR * SPAN), jnp.bfloat16)
         for v in range(2):
             y = 2 * h + v
             for j in range(NNZ):
@@ -152,7 +153,9 @@
             out_ref[:, pl.ds(pl.multiple_of(row * AB, AB), AB)] = part[:, v * AB : (v + 1) * AB]
 
 
-def own_kernel(block_pairs_ref, received_ref, out_ref, pairs_ref, *dense_refs):
+def own_kernel(block_pairs_ref, received_ref, out_ref, pairs_ref, zero0_ref, zero1_ref, *dense_refs):
+    zero0_ref[...] = jnp.zeros((2 * AB, NPAIR * SPAN), jnp.bfloat16)
+    zero1_ref[...] = jnp.zeros((2 * AB, NPAIR * SPAN), jnp.bfloat16)
     for row in range(N_ROW):
         place = jnp.int32(0)
         for k in range(N_COL):
@@ -160,30 +163,33 @@
             pairs_ref[row, place] = jnp.maximum(pair, 0)
             place = jnp.minimum(place + (pair >= 0).astype(jnp.int32), N_COL - 1)
     core = lax.axis_index("c").astype(jnp.int32)
-    chi_rows(core, pairs_ref, received_ref, received_ref, out_ref, dense_refs)
-
-
-def other_kernel(pairs_ref, received_ref, named_ref, part_ref, out_ref, *dense_refs):
-    del part_ref
+    chi_rows(core, pairs_ref, received_ref, received_ref, out_ref, dense_refs, True)
+
+
+def other_kernel(
+    pairs_ref, received_ref, named_ref, part_ref, zero0_ref, zero1_ref, out_ref, *dense_refs
+):
+    del part_ref, zero0_ref, zero1_ref
     core = lax.axis_index("c").astype(jnp.int32)
-    chi_rows(1 - core, pairs_ref, received_ref, named_ref, out_ref, dense_refs)
+    chi_rows(1 - core, pairs_ref, received_ref, named_ref, out_ref, dense_refs, False)
 
 
 def chi_half(kernel, name, *operands):
     first = len(operands) == 2
     part = jax.ShapeDtypeStruct((ROWS, N_ROW * AB), jnp.bfloat16)
     table = jax.ShapeDtypeStruct((N_ROW, N_COL), jnp.int32)
+    dense = [jax.ShapeDtypeStruct((2 * AB, NPAIR * SPAN), jnp.bfloat16)] * 2
     return pl.pallas_call(
         kernel,
-        out_shape=(part, table) if first else part,
+        out_shape=(part, table, *dense) if first else (part, *dense),
         grid_spec=pltpu.PrefetchScalarGridSpec(
             num_scalar_prefetch=1,
             grid=(),
             in_specs=[VMEM] * (len(operands) - 1),
-            out_specs=(VMEM, SMEM) if first else VMEM,
-            scratch_shapes=[pltpu.VMEM((2 * AB, NPAIR * SPAN), jnp.bfloat16)] * 2,
+            out_specs=(VMEM, SMEM, VMEM, VMEM) if first else (VMEM,) * 3,
+            scratch_shapes=[pltpu.VMEM((2 * AB, NPAIR * SPAN), jnp.bfloat16)] * (2 if first else 0),
         ),
-        input_output_aliases={} if first else {3: 0},
+        input_output_aliases={} if first else {3: 0, 4: 1, 5: 2},
         cost_estimate=pl.CostEstimate(
             flops=ROWS * N_ROW * AB * NPAIR * SPAN, bytes_accessed=8 * MIB, transcendentals=0
         ),
@@ -202,8 +208,8 @@
     received = received.reshape(ROWS, WIDTH)
     own = received[:, :NAMED]
     other = lax.ppermute(own, "c", [(0, 1), (1, 0)])
-    part, pairs = chi_half(own_kernel, "chi_own", block_pairs, received)
-    part = chi_half(other_kernel, "chi_other", pairs, received, other, part)
+    part, pairs, *zeros = chi_half(own_kernel, "chi_own", block_pairs, received)
+    part = chi_half(other_kernel, "chi_other", pairs, received, other, part, *zeros)[0]
     part = lax.all_to_all(part.reshape(NCHIP, AUX, N_ROW * AB), chips, 0, 0, tiled=True)
     part, chi_mask = lax.optimization_barrier((part, chi_mask))
     chi = jnp.sum(part.astype(jnp.float32), axis=0)

time: 188 us -> 188 us (level)
  no operation moved by 1% of the time
where the time goes in v6:
time: 188 us; the launch traced here: 187 us
  blocking collectives  170 us (90%)
  Pallas kernels  15.9 us (8%)
    all_to_all x1, blocking collectives, on_device(): lax.all_to_all(sent.reshape(NCHIP, AUX, WIDTH), chips, 0, 0, tiled=True)  87.1 us
    all_to_all x1, blocking collectives, on_device(): lax.all_to_all(x_slots[0, 0].reshape(N_COL, AUX, B, B), ('x', 'z'), 0, 0,...  58.9 us
    all_to_all x1, blocking collectives, on_device(): lax.all_to_all(part.reshape(NCHIP, AUX, N_ROW * AB), chips, 0, 0, tiled=T...  23.6 us
    pallas_call x1, Pallas kernels, slices(): pl.pallas_call(slices_kernel, out_shape=jax.ShapeDtypeStruct((ROWS, WIDTH...  8.51 us
    pallas_call x2, Pallas kernels, chi_half(): pl.pallas_call(kernel, out_shape=(part, table, *dense) if first else (par...  7.44 us
  transfers between devices with their start and end apart: 1, of which 1 were waited for; matrix products, arithmetic and copies ran while one was open for 0% of the time, Pallas kernels for 2%

profile of v6, /device:TPU:0, one launch (start us, length us, event | category | flops | bytes accessed | tf_op | source)
XLA Modules:
  0.0 187.5 jit_solution(5221555286408764382)
XLA Ops:
  0.0 0.0 copy-start
  0.0 0.0 copy-start.1
  0.0 0.0 copy-start.2
  0.0 58.9 %all_to_all.15.arrived_ref = bf16[16,8,128,128]{3,2,1,0:T(8,128)(2,1)S(1)} all-to-all(bf16[16,8,128,128]{3,2,1,0:T(8,128)(2,1)} %bitcast.13), channel_id=1, replica_groups=mesh['y'=4,'c'=2,'x'=4,'z'=4] {'x','z'}, dimensions={0} | all-to-all | bytes 8388608 | tf_op jit(solution)/shard_map/all_to_all | solution.py:203
  58.9 0.0 copy-done
  58.9 0.0 copy-done.1
  58.9 0.0 copy-done.2
  58.9 8.5 %slices.1 = bf16[512,6656]{1,0:T(8,128)(2,1)S(1)} custom-call(s32[8,16]{1,0:T(8,128)S(1)} %copy-done.2, s32[2,4,4]{2,1,0:T(4,128)S(1)} %copy-done.1, bf16[16,8,128,128]{3,2,1,0:T(8,128)(2,1)S(1)} %all_to_all.15.arrived_ref, bf16[2,512,512]{2,1,0:T(8,128)(2,1)S(1)} %copy-done), custom_call_target="tpu_custom_call" | custom-call | tf_op jit(solution)/shard_map/slices/pallas_call | solution.py:112
  67.4 87.1 %all_to_all.16 = bf16[64,8,6656]{2,1,0:T(8,128)(2,1)S(1)} all-to-all(bf16[64,8,6656]{2,1,0:T(8,128)(2,1)S(1)} %bitcast.11), channel_id=1, replica_groups=mesh['y'=4,'c'=2,'x'=4,'z'=4] {'y','x','z'}, dimensions={0} | all-to-all | bytes 13631488 | tf_op jit(solution)/shard_map/all_to_all | solution.py:207
  154.5 0.2 slice.4
  154.7 0.1 collective-permute-start
  154.7 4.2 %chi_own.1 = (bf16[512,1024]{1,0:T(8,128)(2,1)S(1)}, s32[8,16]{1,0:T(8,128)S(1)}, bf16[256,4096]{1,0:T(8,128)(2,1)S(1)}, bf16[256,4096]{1,0:T(8,128)(2,1)S(1)}) custom-call(s32[8,16]{1,0:T(8,128)S(1)} %copy-done.2, bf16[512,6656]{1,0:T(8,128)(2,1)S(1)} %bitcast.9), custom_call_target="tpu_custom_call" | custom-call | flops 2147483648 | bytes 8388608 | tf_op jit(solution)/shard_map/chi_own/pallas_call | solution.py:182
  158.9 0.7 collective-permute-done.named_ref
  159.6 3.3 %chi_other.1 = (bf16[512,1024]{1,0:T(8,128)(2,1)S(1)}, bf16[256,4096]{1,0:T(8,128)(2,1)S(1)}, bf16[256,4096]{1,0:T(8,128)(2,1)S(1)}) custom-call(s32[8,16]{1,0:T(8,128)S(1)} %get-tuple-element.12.pairs_ref, bf16[512,6656]{1,0:T(8,128)(2,1)S(1)} %bitcast.10, ...), custom_call_target="tpu_custom_call", output_to_operand_aliasing={{0}: (3, {}), {1}: (4, {}), {2}: (5, {})} | custom-call | flops 2147483648 | bytes 8388608 | tf_op jit(solution)/shard_map/chi_other/pallas_call | solution.py:182
  162.9 0.0 copy-start.3
  162.9 23.6 %all_to_all.17 = bf16[64,8,1024]{2,1,0:T(8,128)(2,1)S(1)} all-to-all(bf16[64,8,1024]{2,1,0:T(8,128)(2,1)S(1)} %bitcast.12), channel_id=1, replica_groups=mesh['y'=4,'c'=2,'x'=4,'z'=4] {'y','x','z'}, dimensions={0} | all-to-all | bytes 2097152 | tf_op jit(solution)/shard_map/all_to_all | solution.py:213
  186.6 0.2 convert_reduce_fusion
  186.7 0.0 copy-done.3
  186.8 0.1 broadcast_bitcast_fusion
  186.8 0.6 broadcast_multiply_fusion
  (1 shorter events, 0.0 us)
Async XLA Ops:
  0.0 58.9 %copy-start = (bf16[2,512,512]{2,1,0:T(8,128)(2,1)S(1)}, bf16[2,512,512]{2,1,0:T(8,128)(2,1)}, u32[]{:S(2)}) copy-start(bf16[2,512,512]{2,1,0:T(8,128)(2,1)} %greens_ref.1) | copy-start | bytes 3145732
  0.0 58.9 %copy-start.1 = (s32[2,4,4]{2,1,0:T(4,128)S(1)}, s32[2,4,4]{2,1,0:T(4,128)}, u32[]{:S(2)}) copy-start(s32[2,4,4]{2,1,0:T(4,128)} %mask_ref.1) | copy-start | bytes 388
  0.0 58.9 %copy-start.2 = (s32[8,16]{1,0:T(8,128)S(1)}, s32[8,16]{1,0:T(8,128)}, u32[]{:S(2)}) copy-start(s32[8,16]{1,0:T(8,128)} %block_pairs_ref.3) | copy-start | bytes 1540
  154.7 5.0 %collective-permute-start = (bf16[512,2560]{1,0:T(8,128)(2,1)S(1)}, bf16[512,2560]{1,0:T(8,128)(2,1)S(1)}, u32[]{:S(2)}, u32[]{:S(2)}) collective-permute-start(bf16[512,2560]{1,0:T(8,128)(2,1)S(1)} %slice.4), channel_id=1, source_target_pairs={{0,16},{16,0},{1,17},{17,1},{2,18},{18,2},{3,19},{19,3},{4,20},{20... | collective-permute-start | bytes 7864328 | tf_op jit(solution)/shard_map/ppermute | solution.py:210
  162.9 23.8 %copy-start.3 = (s32[1,8]{1,0:T(1,128)S(1)}, s32[1,8]{1,0:T(1,128)}, u32[]{:S(2)}) copy-start(s32[1,8]{1,0:T(1,128)} %param.9) | copy-start | bytes 100
